TPU v7x, 128 devices: a whole 4x4x4 slice. The times are simulated.
128 devices in a mesh: row: 8 (over z, y_lo), col: 16 (over y_hi, x, core).
Axes of the slice: x: 4, y: 4 (y_hi: 2, y_lo: 2; y = y_hi * 2 + y_lo), z: 4, core: 2. Of those that a mesh axis runs over, the one named last changes fastest.
Arguments:
- orbitals: bfloat16 [32, 64, 512], P('row', 'col'), may hold values from -6 to 6
- screened: bfloat16 [16384, 512], P(('row', 'col')), may hold values from -2.1579186e-05 to 2.1579186e-05
- kpoints: int32 [32], replicated, may hold values from 0 to 31, each once
- vectors: bfloat16 [64, 32768], P(None, ('row', 'col')), may hold values from -6 to 6
- energies: float32 [32, 64], replicated, may hold values from -1 to 1
Outputs:
- filtered: float32 [64, 32768], P(None, ('row', 'col'))
All inputs are finite; a program needn't handle non-finite values.
Results may differ from a plain program's by a relative error of at most 0.0034.
Values may be sent and summed in bfloat16 or wider, within the bound.
A program may use at most 128 MiB of HBM per device.

v0:
```python
import jax
import jax.numpy as jnp
from jax import lax
from jax.sharding import PartitionSpec as P

NV = 32
NC = 32
NG = 512


SPREAD = 4.0


def sent_to_all(x, axis):
    length = lax.axis_size(axis)
    return lax.all_to_all(jnp.broadcast_to(x[None], (length, *x.shape)), axis, 0, 0, tiled=True)


def joined_along(pieces, dim):
    pieces = jnp.moveaxis(pieces, 0, dim)
    lengths = pieces.shape
    return pieces.reshape(*lengths[:dim], lengths[dim] * lengths[dim + 1], *lengths[dim + 2 :])


def collect(x, axis, dim):
    pieces = sent_to_all(x, axis)
    return joined_along(pieces, dim)


def from_root(x, axis, root):
    return lax.dynamic_index_in_dim(lax.all_gather(x, axis), root, 0, keepdims=False)


def pair_tile(orbit_left, orbit_right, screen_block):
    valence = (
        orbit_left[:NV].astype(jnp.float32)[:, None, :]
        * orbit_right[:NV].astype(jnp.float32)[None, :, :]
    )
    conduct = (
        orbit_left[NV:].astype(jnp.float32)[:, None, :]
        * orbit_right[NV:].astype(jnp.float32)[None, :, :]
    )
    valence = valence.reshape(NV * NV, NG).astype(jnp.bfloat16)
    conduct = conduct.reshape(NC * NC, NG).astype(jnp.bfloat16)
    amplitude = jnp.dot(valence, screen_block, preferred_element_type=jnp.float32).astype(
        jnp.bfloat16
    )
    inner_tile = jnp.dot(amplitude, conduct.T, preferred_element_type=jnp.float32)
    inner_tile = inner_tile.reshape(NV, NV, NC, NC).transpose(0, 2, 1, 3)
    return inner_tile.reshape(NV * NC, NV * NC).astype(jnp.bfloat16)


def per_device(orbitals, screened, kpoints, vectors, energies):
    row_count = lax.axis_size("row")
    col_count = lax.axis_size("col")
    row_index = lax.axis_index("row")
    col_index = lax.axis_index("col")
    col_ratio = col_count // row_count
    points = kpoints.shape[0]
    row_points = points // row_count
    col_points = points // col_count
    pair_count = NV * NC
    local_width = vectors.shape[1]
    block_width = col_points * pair_count
    root_row = col_index // col_ratio
    half_index = col_index % col_ratio
    row_orbits = collect(orbitals, "col", 1)
    own_part = lax.dynamic_slice_in_dim(row_orbits, half_index * col_points, col_points, 0)
    col_orbits = from_root(own_part, "row", root_row)
    gap_full = (energies[:, NV:][:, None, :] - energies[:, :NV][:, :, None]).reshape(
        points * pair_count
    )
    screen_all = lax.all_gather(screened, ("row", "col"), axis=0, tiled=True)

    def build_tile(tile_index):
        left_slot = tile_index // col_points
        right_slot = tile_index % col_points
        left_point = kpoints[row_index * row_points + left_slot]
        right_point = kpoints[col_index * col_points + right_slot]
        momentum = (left_point - right_point + points) % points
        screen_block = lax.dynamic_slice_in_dim(screen_all, momentum * NG, NG, 0)
        return pair_tile(row_orbits[left_slot], col_orbits[right_slot], screen_block)

    kernel_tiles = lax.map(build_tile, jnp.arange(row_points * col_points, dtype=jnp.int32))
    kernel_tiles = kernel_tiles.reshape(row_points, col_points, pair_count, pair_count)

    def apply_tiles(column_vectors):
        shaped = column_vectors.reshape(column_vectors.shape[0], col_points, pair_count)
        product = jnp.einsum(
            "nbs,abrs->nar", shaped, kernel_tiles, preferred_element_type=jnp.float32
        )
        return product.reshape(column_vectors.shape[0], row_points * pair_count)

    gap_here = lax.dynamic_slice_in_dim(
        gap_full, row_index * row_points * pair_count, row_points * pair_count, 0
    )

    def applied(rounded):
        half_block = lax.dynamic_slice_in_dim(rounded, half_index * block_width, block_width, 1)
        column_vectors = from_root(half_block, "row", root_row)
        return lax.psum(apply_tiles(column_vectors), "col")

    first_rounded = collect(vectors, "col", 1)

    def hamilton(current, rounded):
        return (gap_here * current + applied(rounded)) / SPREAD

    state_first = first_rounded.astype(jnp.float32)
    second = hamilton(state_first, first_rounded)
    state_third = 2.0 * hamilton(second, second.astype(jnp.bfloat16)) - state_first
    result = 2.0 * hamilton(state_third, state_third.astype(jnp.bfloat16)) - second
    result = lax.dynamic_slice_in_dim(result, col_index * local_width, local_width, 1)
    return result


def solution(mesh):
    placed = (P("row", "col", None), P(("row", "col"), None), P(), P(None, ("row", "col")), P())
    return jax.shard_map(
        per_device, mesh=mesh, in_specs=placed, out_specs=P(None, ("row", "col")), check_vma=False
    )
```

profile of v0, /device:TPU:0, one launch (start us, length us, event | category | flops | bytes accessed | tf_op | source)
XLA Modules:
  0.0 1150.0 jit_solution(7976291049981896924)
XLA Ops:
  8.1 7.1 all-to-all-start.1
  15.2 9.3 all-to-all-done.1
  30.8 12.3 %all-to-all-done = bf16[16,64,256]{2,1,0:T(8,128)(2,1)S(1)} async-done(((bf16[16,64,256]{2,1,0:T(8,128)(2,1)}), bf16[16,64,256]{2,1,0:T(8,128)(2,1)S(1)}, u32[]{:S(2)}, u32[]{:S(2)}) %all-to-all-start) | async-done | bytes 524320 | tf_op jit(solution)/shard_map/all_to_all | solution.py:16
  44.8 22.2 %all-gather.14.cloned.1.call-done = bf16[16,64,512]{2,1,0:T(8,128)(2,1)} async-done(((bf16[2,64,512]{2,1,0:T(8,128)(2,1)}), bf16[16,64,512]{2,1,0:T(8,128)(2,1)}) %all-gather.14.cloned.1.call-update) | async-done | bytes 1048592 | tf_op jit(solution)/shard_map/all_gather | solution.py:31
  67.9 54.4 %all-gather.12.cloned.1.call-done = bf16[512,2048]{1,0:T(8,128)(2,1)} async-done(((bf16[64,2048]{1,0:T(8,128)(2,1)}), bf16[512,2048]{1,0:T(8,128)(2,1)}) %all-gather.12.cloned.1.call-update) | async-done | bytes 2097168 | tf_op jit(solution)/shard_map/all_gather | solution.py:31
  123.5 213.9 %all-gather.10.cloned.1.call-done = bf16[16384,512]{1,0:T(8,128)(2,1)} async-done(((bf16[128,512]{1,0:T(8,128)(2,1)}), bf16[16384,512]{1,0:T(8,128)(2,1)}) %all-gather.10.cloned.1.call-update) | async-done | bytes 16777232 | tf_op jit(solution)/shard_map/all_gather | solution.py:73
  337.4 222.5 %while.13 = (s32[]{:T(128)}, bf16[8,1024,1024]{2,1,0:T(8,128)(2,1)}, s32[8]{0:T(128)S(1)}, bf16[4,64,512]{2,1,0:T(8,128)(2,1)S(1)}, bf16[2,64,512]{2,1,0:T(8,128...) while((s32[]{:T(128)}, ...), condition=%wide.region_1.2_spmd, body=%wide.region_0.1_spmd.sunk | while | flops 1614348288 | bytes 15860995 | solution.py:84
  352.4 11.3 convert_element_type.125
  380.2 11.3 convert_element_type.125
  407.9 11.3 convert_element_type.125
  435.7 11.3 convert_element_type.125
  463.6 11.3 convert_element_type.125
  491.5 11.3 convert_element_type.125
  519.3 11.3 convert_element_type.125
  547.1 11.3 convert_element_type.125
  559.9 13.8 %copy.20 = bf16[4,1024,2,1024]{3,1,0,2:T(8,128)(2,1)} copy(bf16[4,1024,2,1024]{3,1,2,0:T(8,128)(2,1)} %bitcast.83) | data formatting | bytes 33554432 | tf_op jit(solution)/shard_map/nbs,abrs->nar/dot_general | solution.py:89
  573.7 12.0 %convolution_bitcast_fusion.2 = f32[64,4096]{1,0:T(8,128)} fusion(bf16[4096,2,1024]{2,0,1:T(8,128)(2,1)} %bitcast.79, bf16[64,2,1024]{2,1,0:T(2,128)(2,1)S(1)} %reshape.105), kind=kOutput, calls=%fused_computation.20 | convolution fusion | flops 1073741824 | bytes 18087936 | tf_op jit(solution)/shard_map/nbs,abrs->nar/dot_general | solution.py:89
  586.3 138.4 %all-reduce.4.cloned.1.call-done = f32[64,4096]{1,0:T(8,128)} async-done(((f32[64,4096]{1,0:T(8,128)}), f32[64,4096]{1,0:T(8,128)}) %all-reduce.4.cloned.1.call-update) | async-done | bytes 1048592 | tf_op jit(solution)/shard_map/psum | solution.py:101
  727.2 53.3 %all-gather.16.cloned.1.call-done = bf16[512,2048]{1,0:T(8,128)(2,1)} async-done(((bf16[64,2048]{1,0:T(8,128)(2,1)}), bf16[512,2048]{1,0:T(8,128)(2,1)}) %all-gather.16.cloned.1.call-update) | async-done | bytes 2097168 | tf_op jit(solution)/shard_map/all_gather | solution.py:31
  781.6 11.9 %convolution_bitcast_fusion.1 = f32[64,4096]{1,0:T(8,128)} fusion(bf16[4096,2,1024]{2,0,1:T(8,128)(2,1)} %bitcast.80, bf16[64,2,1024]{2,1,0:T(2,128)(2,1)S(1)} %reshape.108), kind=kOutput, calls=%fused_computation.19 | convolution fusion | flops 1073741824 | bytes 18087936 | tf_op jit(solution)/shard_map/nbs,abrs->nar/dot_general | solution.py:89
  793.6 139.5 %all-reduce.6.cloned.1.call-done = f32[64,4096]{1,0:T(8,128)} async-done(((f32[64,4096]{1,0:T(8,128)}), f32[64,4096]{1,0:T(8,128)}) %all-reduce.6.cloned.1.call-update) | async-done | bytes 1048592 | tf_op jit(solution)/shard_map/psum | solution.py:101
  935.4 53.5 %all-gather.18.cloned.1.call-done = bf16[512,2048]{1,0:T(8,128)(2,1)} async-done(((bf16[64,2048]{1,0:T(8,128)(2,1)}), bf16[512,2048]{1,0:T(8,128)(2,1)}) %all-gather.18.cloned.1.call-update) | async-done | bytes 2097168 | tf_op jit(solution)/shard_map/all_gather | solution.py:31
  990.1 12.0 %convolution_bitcast_fusion = f32[64,4096]{1,0:T(8,128)} fusion(bf16[4096,2,1024]{2,0,1:T(8,128)(2,1)} %bitcast.81, bf16[64,2,1024]{2,1,0:T(2,128)(2,1)S(1)} %reshape.109), kind=kOutput, calls=%fused_computation.18 | convolution fusion | flops 1073741824 | bytes 18087936 | tf_op jit(solution)/shard_map/nbs,abrs->nar/dot_general | solution.py:89
  1002.1 139.5 %all-reduce.8.cloned.1.call-done = f32[64,4096]{1,0:T(8,128)} async-done(((f32[64,4096]{1,0:T(8,128)}), f32[64,4096]{1,0:T(8,128)}) %all-reduce.8.cloned.1.call-update) | async-done | bytes 1048592 | tf_op jit(solution)/shard_map/psum | solution.py:101
  (106 shorter events, 121.1 us)
Async XLA Ops:
  8.1 16.5 %all-to-all-start.1 = ((bf16[16,4,4,512]{3,2,1,0:T(4,128)(2,1)}), bf16[16,4,4,512]{3,2,1,0:T(4,128)(2,1)S(1)}, u32[]{:S(2)}, u32[]{:S(2)}) async-start(bf16[16,4,4,512]{3,2,1,0:T(4,128)(2,1)} %broadcast_in_dim.9), calls=%async_computation.1 | async-start | bytes 524288 | tf_op jit(solution)/shard_map/all_to_all | solution.py:16
  15.2 51.8 %all-gather.14.cloned.1.call-start = ((), (), s32[]{:S(2)}) async-start(), calls=%async_computation.7 | async-start | bytes 1179648 | tf_op jit(solution)/shard_map/all_gather | solution.py:31
  27.1 15.9 %all-to-all-start = ((bf16[16,64,256]{2,1,0:T(8,128)(2,1)}), bf16[16,64,256]{2,1,0:T(8,128)(2,1)S(1)}, u32[]{:S(2)}, u32[]{:S(2)}) async-start(bf16[16,64,256]{2,1,0:T(8,128)(2,1)} %broadcast_in_dim.7), calls=%async_computation | async-start | bytes 1048576 | tf_op jit(solution)/shard_map/all_to_all | solution.py:16
  30.7 91.6 %all-gather.12.cloned.1.call-start = ((), (), s32[]{:S(2)}) async-start(), calls=%async_computation.6 | async-start | bytes 2359296 | tf_op jit(solution)/shard_map/all_gather | solution.py:31
  43.9 293.5 %all-gather.10.cloned.1.call-start = ((), (), s32[]{:S(2)}) async-start(), calls=%async_computation.2 | async-start | bytes 16908288 | tf_op jit(solution)/shard_map/all_gather | solution.py:73
  44.6 680.0 %all-reduce.4.cloned.1.call-start = ((), (), s32[]{:S(2)}) async-start(), calls=%async_computation.3 | async-start | bytes 2097152 | tf_op jit(solution)/shard_map/psum | solution.py:101
  573.7 12.1 %copy-start.2 = (f32[32,64]{1,0:T(8,128)S(1)}, f32[32,64]{1,0:T(8,128)}, u32[]{:S(2)}) copy-start(f32[32,64]{1,0:T(8,128)} %param.11) | copy-start | bytes 24580
  585.7 194.7 %all-gather.16.cloned.1.call-start = ((), (), s32[]{:S(2)}) async-start(), calls=%async_computation.8 | async-start | bytes 2359296 | tf_op jit(solution)/shard_map/all_gather | solution.py:31
  724.6 208.5 %copy-start = (f32[64,4096]{1,0:T(8,128)S(1)}, f32[64,4096]{1,0:T(8,128)}, u32[]{:S(2)}) copy-start(f32[64,4096]{1,0:T(8,128)} %all-reduce.4.cloned.1.call-done) | copy-start | bytes 3145732
  726.1 207.0 %copy-start.1 = (f32[64,4096]{1,0:T(8,128)}, f32[64,4096]{1,0:T(8,128)S(1)}, u32[]{:S(2)}) copy-start(f32[64,4096]{1,0:T(8,128)S(1)} %fusion.11) | copy-start | bytes 3145732
  726.9 206.2 %all-reduce.6.cloned.1.call-start = ((), (), s32[]{:S(2)}) async-start(), calls=%async_computation.4 | async-start | bytes 2097152 | tf_op jit(solution)/shard_map/psum | solution.py:101
  793.5 195.4 %all-gather.18.cloned.1.call-start = ((), (), s32[]{:S(2)}) async-start(), calls=%async_computation.9 | async-start | bytes 2359296 | tf_op jit(solution)/shard_map/all_gather | solution.py:31
  935.4 206.2 %all-reduce.8.cloned.1.call-start = ((), (), s32[]{:S(2)}) async-start(), calls=%async_computation.5 | async-start | bytes 2097152 | tf_op jit(solution)/shard_map/psum | solution.py:101
Sparse Core Ops, SparseCore 0:
  25.6 41.2 all-gather.13
  68.6 53.6 all-gather.11
  124.1 213.2 all-gather.9
  585.9 138.7 all-reduce.3
  727.0 53.3 all-gather.15
  793.7 139.3 all-reduce.5
  935.5 53.3 all-gather.17
  1002.2 139.4 all-reduce.7
where the time goes:
time: 1150 us
  waiting for transfers between devices  837 us (73%)
  local copies, waits for them, and re-layouts  144 us (13%)
  matrix products  106 us (9%)
  loops' own time  31.5 us (3%)
  between operations  13.7 us (1%)
    psum x3, waiting for transfers between devices, applied(): return lax.psum(apply_tiles(column_vectors), 'col')  417 us
    all_gather x1, waiting for transfers between devices, per_device(): screen_all = lax.all_gather(screened, ('row', 'col'), axis=0, tiled=True)  214 us
    all_gather x4, waiting for transfers between devices, from_root(): lax.all_gather(x, axis)  183 us
    convert_element_type x8, local copies, waits for them, and re-layouts, pair_tile(): return inner_tile.reshape(NV * NC, NV * NC).astype(jnp.bfloat16)  90.6 us
    dot_general x8, matrix products, pair_tile(): jnp.dot(amplitude, conduct.T, preferred_element_type=jnp.float32)  55.8 us
    dot_general x3, matrix products, apply_tiles(): jnp.einsum('nbs,abrs->nar', shaped, kernel_tiles, preferred_element_type=...  35.8 us
    another operation x1, loops' own time, per_device(): lax.map(build_tile, jnp.arange(row_points * col_points, dtype=jnp.int32))  31.5 us
  transfers between devices with their start and end apart: 10, of which 10 were waited for; matrix products, arithmetic and copies ran while one was open for 0% of the time, Pallas kernels for 0%

commit v1 on v0

v1 whole, which is shorter than its diff:
```python
import jax
import jax.numpy as jnp
from jax import lax
from jax.experimental import pallas as pl
from jax.experimental.pallas import tpu as pltpu
from jax.sharding import PartitionSpec as P

NV = 32
NC = 32
NG = 512
NX = 64
NK = 32
PAIRS = NV * NC
ROWS = 8
COLS = 16
SPREAD = 4.0


def column_value(col, t):
    return col // 2 + 8 * lax.rem(col, 2) + 16 * t


def remote(src, dst, send_sem, recv_sem, row, col):
    return pltpu.make_async_remote_copy(
        src_ref=src,
        dst_ref=dst,
        send_sem=send_sem,
        recv_sem=recv_sem,
        device_id=(row, col),
        device_id_type=pl.DeviceIdType.MESH,
    )


def gather_kernel(
    place,
    orb_ref,
    screen_ref,
    vec_ref,
    orb_out,
    screen_out,
    vec_out,
    own_out,
    orb_all,
    staged,
    landed,
    wide,
    vec_all,
    vec_staged,
    s1,
    r1,
    s2,
    r2,
    sw,
    rw,
    lw,
    sv,
    rv,
    sx,
    rx,
):
    a = lax.axis_index("row")
    b = lax.axis_index("col")
    quarter = lax.rem(b, 4)
    group = b // 4

    def first_copy(d):
        return remote(
            orb_ref,
            orb_all.at[pl.ds(4 * a, 4)],
            s1.at[d],
            r1.at[d],
            lax.rem(a + d + 1, ROWS),
            b,
        )

    @pl.loop(0, ROWS - 1)
    def _(d):
        first_copy(d).start()

    orb_all[pl.ds(4 * a, 4)] = orb_ref[...]

    residue = lax.rem(4 * lax.rem(a, 2) + group, 8)
    piece = (a // 2) * 4 + quarter

    def screen_target(i):
        row = lax.rem(a + i // 2, ROWS)
        col = 2 * lax.rem(row - residue + 8, 8) + lax.rem(i, 2)
        return row, col

    def screen_copy(i):
        row, col = screen_target(i)
        return remote(screen_ref, screen_out.at[piece], sw.at[i], rw.at[piece], row, col)

    def screen_local():
        return pltpu.make_async_copy(screen_ref, screen_out.at[piece], lw)

    def is_self(i):
        row, col = screen_target(i)
        return jnp.logical_and(row == a, col == b)

    @pl.loop(0, ROWS - 1)
    def _(d):
        first_copy(d).wait()

    @pl.loop(0, COLS)
    def _(dest):
        for m in range(4):
            staged[dest, m] = orb_all[place[a + 8 * m]]
        for t in range(2):
            staged[dest, 4 + t] = orb_all[place[column_value(dest, t)]]

    def second_copy(d):
        col = lax.rem(b + d + 1, COLS)
        return remote(staged.at[col], landed.at[b], s2.at[d], r2.at[d], a, col)

    @pl.loop(0, COLS - 1)
    def _(d):
        second_copy(d).start()

    @pl.loop(0, 16)
    def _(i):
        @pl.when(is_self(i))
        def _():
            screen_local().start()

        @pl.when(jnp.logical_not(is_self(i)))
        def _():
            screen_copy(i).start()

    landed[b] = staged[b]

    mine = a * 4 + group

    def vector_copy(d):
        other = lax.rem(mine + d + 1, NK)
        return remote(
            vec_ref,
            vec_all.at[mine],
            sv.at[d],
            rv.at[d],
            other // 4,
            4 * lax.rem(other, 4) + quarter,
        )

    @pl.loop(0, NK - 1)
    def _(d):
        vector_copy(d).start()

    vec_all[mine] = vec_ref[...]

    @pl.loop(0, COLS - 1)
    def _(d):
        second_copy(d).wait()

    @pl.loop(0, 6)
    def _(slot):
        for source in range(COLS):
            wide[source * 16 : source * 16 + 16] = landed[source, slot].astype(jnp.float32)
        for part in range(4):
            orb_out[slot, :, part * 128 : part * 128 + 128] = wide[pl.ds(part, 64, stride=4), :]

    @pl.loop(0, NK - 1)
    def _(d):
        vector_copy(d).wait()

    own_out[...] = vec_all[place[a + 8 * group]]

    def spread_copy(d):
        col = 4 * group + lax.rem(quarter + d + 1, 4)
        return remote(vec_staged.at[d], vec_out.at[quarter], sx.at[d], rx.at[d], a, col)

    for d in range(3):
        col = 4 * group + lax.rem(quarter + d + 1, 4)
        for t in range(2):
            vec_staged[d, t] = vec_all[place[column_value(col, t)]]
        spread_copy(d).start()
    for t in range(2):
        vec_out[quarter, t] = vec_all[place[column_value(b, t)]]

    needed = lax.rem(a - b // 2 + 8, 8)
    @pl.loop(0, 16)
    def _(p):
        own_piece = jnp.logical_and(needed == residue, p == piece)

        @pl.when(own_piece)
        def _():
            screen_local().wait()

        @pl.when(jnp.logical_not(own_piece))
        def _():
            remote(screen_ref, screen_out.at[p], sw.at[p], rw.at[p], a, lax.rem(b + 1, COLS)).wait_recv()

    @pl.loop(0, 16)
    def _(i):
        @pl.when(jnp.logical_not(is_self(i)))
        def _():
            screen_copy(i).wait_send()

    for d in range(3):
        spread_copy(d).wait()


def gathered(place, orbitals, screened, vectors):
    dma = pltpu.SemaphoreType.DMA
    vmem = pl.BlockSpec(memory_space=pltpu.VMEM)
    return pl.pallas_call(
        gather_kernel,
        out_shape=(
            jax.ShapeDtypeStruct((6, 64, NG), jnp.float32),
            jax.ShapeDtypeStruct((16, 128, NG), jnp.bfloat16),
            jax.ShapeDtypeStruct((4, 2, NX, 256), jnp.bfloat16),
            jax.ShapeDtypeStruct((NX, 256), jnp.bfloat16),
        ),
        in_specs=[pl.BlockSpec(memory_space=pltpu.SMEM), vmem, vmem, vmem],
        out_specs=(vmem, vmem, vmem, vmem),
        scratch_shapes=[
            pltpu.VMEM((NK, 16, 128), jnp.bfloat16),
            pltpu.VMEM((COLS, 6, 16, 128), jnp.bfloat16),
            pltpu.VMEM((COLS, 6, 16, 128), jnp.bfloat16),
            pltpu.VMEM((256, 128), jnp.float32),
            pltpu.VMEM((NK, NX, 256), jnp.bfloat16),
            pltpu.VMEM((3, 2, NX, 256), jnp.bfloat16),
            dma((7,)),
            dma((7,)),
            dma((15,)),
            dma((15,)),
            dma((16,)),
            dma((16,)),
            dma,
            dma((31,)),
            dma((31,)),
            dma((3,)),
            dma((3,)),
        ],
        compiler_params=pltpu.CompilerParams(has_side_effects=True, vmem_limit_bytes=48 << 20),
        name="gather",
    )(place, orbitals, screened, vectors)


def tile_kernel(slots, orb_left, orb_right, screen_ref, out_ref, valence, conduct, amplitude, product):
    pair = pl.program_id(0)
    slot = slots[pair]
    for v in range(NV):
        valence[v * 32 : v * 32 + 32] = (orb_left[0, v : v + 1] * orb_right[0, :NV]).astype(jnp.bfloat16)
        conduct[v * 32 : v * 32 + 32] = (orb_right[0, NV + v : NV + v + 1] * orb_left[0, NV:]).astype(
            jnp.bfloat16
        )
    amplitude[...] = jnp.dot(
        valence[...], screen_ref[slot], preferred_element_type=jnp.float32
    ).astype(jnp.bfloat16)
    lane = lax.broadcasted_iota(jnp.int32, (32, 128), 1)
    low = lane < 64
    even = lax.rem(lane // 32, 2) == 0
    for block in range(4):
        product[...] = lax.dot_general(
            amplitude[...],
            conduct[block * 256 : block * 256 + 256],
            (((1,), (1,)), ((), ())),
            preferred_element_type=jnp.float32,
        )
        for group in range(8):
            for half in range(2):
                s = [
                    product[group * 128 + i * 32 : group * 128 + i * 32 + 32, half * 128 : half * 128 + 128]
                    for i in range(4)
                ]
                u0 = jnp.where(low, s[0], pltpu.roll(s[2], 64, 1))
                u2 = jnp.where(low, pltpu.roll(s[0], 64, 1), s[2])
                u1 = jnp.where(low, s[1], pltpu.roll(s[3], 64, 1))
                u3 = jnp.where(low, pltpu.roll(s[1], 64, 1), s[3])
                t = [
                    jnp.where(even, u0, pltpu.roll(u1, 32, 1)),
                    jnp.where(even, pltpu.roll(u0, 96, 1), u1),
                    jnp.where(even, u2, pltpu.roll(u3, 32, 1)),
                    jnp.where(even, pltpu.roll(u2, 96, 1), u3),
                ]
                first = block * 256 + half * 128
                lanes = (group % 2) * 128
                for i in range(4):
                    out_ref[group // 2, first + i * 32 : first + i * 32 + 32, lanes : lanes + 128] = t[i].astype(
                        jnp.bfloat16
                    )


def tiles(slots, orbitals, screened):
    return pl.pallas_call(
        tile_kernel,
        out_shape=jax.ShapeDtypeStruct((16, 2 * PAIRS, 256), jnp.bfloat16),
        grid_spec=pltpu.PrefetchScalarGridSpec(
            num_scalar_prefetch=1,
            grid=(8,),
            in_specs=[
                pl.BlockSpec((1, 64, NG), lambda i, s: (i // 2, 0, 0)),
                pl.BlockSpec((1, 64, NG), lambda i, s: (4 + i % 2, 0, 0)),
                pl.BlockSpec((4, NG, NG), lambda i, s: (0, 0, 0)),
            ],
            out_specs=pl.BlockSpec((4, PAIRS, 256), lambda i, s: (i // 2, i % 2, 0)),
            scratch_shapes=[
                pltpu.VMEM((PAIRS, NG), jnp.bfloat16),
                pltpu.VMEM((PAIRS, NG), jnp.bfloat16),
                pltpu.VMEM((PAIRS, NG), jnp.bfloat16),
                pltpu.VMEM((PAIRS, 256), jnp.float32),
            ],
        ),
        compiler_params=pltpu.CompilerParams(vmem_limit_bytes=48 << 20),
        name="tiles",
    )(slots, orbitals, orbitals, screened.reshape(4, NG, NG))


def filter_kernel(
    value,
    kern_ref,
    vec_ref,
    own_ref,
    gap_ref,
    out_ref,
    swap,
    column,
    ordered,
    sent,
    got,
    rounded,
    state,
    final_row,
    final_out,
    final_in,
    sp,
    rp,
    sg,
    rg,
    lg,
    sa,
    ra,
    sb,
    rb,
):
    a = lax.axis_index("row")
    b = lax.axis_index("col")
    quarter = lax.rem(b, 4)
    group = b // 4

    @pl.loop(0, 8)
    def _(i):
        row = lax.broadcasted_iota(jnp.int32, (128, PAIRS), 0) + i * 128
        col = lax.broadcasted_iota(jnp.int32, (128, PAIRS), 1)
        source = lax.rem(col, 32) * 32 + col // 32
        swap[pl.ds(pl.multiple_of(i * 128, 128), 128)] = jnp.where(row == source, 1.0, 0.0).astype(jnp.bfloat16)

    owner_col = 2 * a + lax.rem(group, 2)
    owner_slot = group // 2
    mine = own_ref[...].astype(jnp.float32)
    gap = gap_ref[...]

    def partial_copy(step, d):
        col = lax.rem(b + d + 1, COLS)
        return remote(sent.at[step, d], got.at[step, b], sp.at[step, d], rp.at[step, d], a, col)

    def spread_target(i):
        row = lax.rem(a + i, ROWS)
        return row, jnp.logical_and(row == a, owner_col == b)

    def spread_copy(step, i):
        row, _ = spread_target(i)
        return remote(
            rounded.at[step],
            column.at[step, owner_slot * 4 + quarter],
            sg.at[step, i],
            rg.at[step, owner_slot * 4 + quarter],
            row,
            owner_col,
        )

    for step in range(3):
        for t in range(2):
            block = jnp.zeros((NX, PAIRS), jnp.float32)
            for j in range(4):
                part = vec_ref[j, t] if step == 0 else column[step - 1, t * 4 + j]
                block += jnp.dot(
                    part, swap[j * 256 : j * 256 + 256], preferred_element_type=jnp.float32
                )
            ordered[:, t * PAIRS : t * PAIRS + PAIRS] = block.astype(jnp.bfloat16)

        @pl.loop(0, COLS)
        def _(d):
            col = lax.rem(b + d + 1, COLS)
            part = jnp.dot(ordered[...], kern_ref[col], preferred_element_type=jnp.float32)
            sent[step, d] = part.astype(jnp.bfloat16)

            @pl.when(d < COLS - 1)
            def _():
                partial_copy(step, d).start()

        @pl.loop(0, COLS - 1)
        def _(d):
            partial_copy(step, d).wait()

        got[step, b] = sent[step, COLS - 1]
        total = jnp.zeros((NX, 256), jnp.float32)
        for source in range(COLS):
            total += got[step, source].astype(jnp.float32)
        if step == 0:
            second = (gap * mine + total) / SPREAD
            state[0] = second
            new = second
        elif step == 1:
            third = 2.0 * ((gap * state[0] + total) / SPREAD) - mine
            state[1] = third
            new = third
        else:
            new = 2.0 * ((gap * state[1] + total) / SPREAD) - state[0]
        if step < 2:
            rounded[step] = new.astype(jnp.bfloat16)

            @pl.loop(0, ROWS)
            def _(i):
                _, here = spread_target(i)

                @pl.when(here)
                def _():
                    pltpu.make_async_copy(
                        rounded.at[step], column.at[step, owner_slot * 4 + quarter], lg.at[step]
                    ).start()

                @pl.when(jnp.logical_not(here))
                def _():
                    spread_copy(step, i).start()

            @pl.loop(0, 8)
            def _(p):
                owner = b // 2
                owner_group = lax.rem(b, 2) + 2 * (p // 4)
                here = jnp.logical_and(owner == a, 4 * owner_group + lax.rem(p, 4) == b)

                @pl.when(here)
                def _():
                    pltpu.make_async_copy(rounded.at[step], column.at[step, p], lg.at[step]).wait()

                @pl.when(jnp.logical_not(here))
                def _():
                    remote(
                        rounded.at[step],
                        column.at[step, p],
                        sg.at[step, p],
                        rg.at[step, p],
                        lax.rem(a + 1, ROWS),
                        b,
                    ).wait_recv()
        else:
            final_row[group] = new

    def row_copy(d):
        col = lax.rem(b + 4 * (d + 1), COLS)
        return remote(final_row.at[group], final_row.at[group], sa.at[d], ra.at[d], a, col)

    for d in range(3):
        row_copy(d).start()
    for step in range(2):

        @pl.loop(0, ROWS)
        def _(i):
            _, here = spread_target(i)

            @pl.when(jnp.logical_not(here))
            def _():
                spread_copy(step, i).wait_send()

    for d in range(3):
        row_copy(d).wait()

    def last_copy(d):
        return remote(
            final_out.at[d], final_in.at[a], sb.at[d], rb.at[d], lax.rem(a + d + 1, ROWS), b
        )

    for d in range(7):
        final_out[d] = final_row[value[4 * lax.rem(a + d + 1, ROWS) + group] // 8]
        last_copy(d).start()
    final_in[a] = final_row[value[4 * a + group] // 8]
    for d in range(7):
        last_copy(d).wait()
    out_ref[...] = final_in[lax.rem(value[4 * a + group], 8)]


def filtered(value, kernel_tiles, vectors, own, gap):
    dma = pltpu.SemaphoreType.DMA
    vmem = pl.BlockSpec(memory_space=pltpu.VMEM)
    return pl.pallas_call(
        filter_kernel,
        out_shape=jax.ShapeDtypeStruct((NX, 256), jnp.float32),
        in_specs=[pl.BlockSpec(memory_space=pltpu.SMEM), vmem, vmem, vmem, vmem],
        out_specs=vmem,
        scratch_shapes=[
            pltpu.VMEM((PAIRS, PAIRS), jnp.bfloat16),
            pltpu.VMEM((2, 8, NX, 256), jnp.bfloat16),
            pltpu.VMEM((NX, 2 * PAIRS), jnp.bfloat16),
            pltpu.VMEM((3, COLS, NX, 256), jnp.bfloat16),
            pltpu.VMEM((3, COLS, NX, 256), jnp.bfloat16),
            pltpu.VMEM((2, NX, 256), jnp.bfloat16),
            pltpu.VMEM((2, NX, 256), jnp.float32),
            pltpu.VMEM((4, NX, 256), jnp.float32),
            pltpu.VMEM((7, NX, 256), jnp.float32),
            pltpu.VMEM((8, NX, 256), jnp.float32),
            dma((3, 15)),
            dma((3, 15)),
            dma((2, 8)),
            dma((2, 8)),
            dma((2,)),
            dma((3,)),
            dma((3,)),
            dma((7,)),
            dma((7,)),
        ],
        compiler_params=pltpu.CompilerParams(has_side_effects=True, vmem_limit_bytes=56 << 20),
        name="filter",
    )(value, kernel_tiles, vectors, own, gap)


def per_device(orbitals, screened, kpoints, vectors, energies):
    a = lax.axis_index("row")
    b = lax.axis_index("col")
    points = jnp.arange(NK, dtype=jnp.int32)
    place = jnp.sum(jnp.where(kpoints[None, :] == points[:, None], points[None, :], 0), axis=1, dtype=jnp.int32)
    orb, screen, column, own = gathered(place, orbitals.reshape(4, 16, 128), screened, vectors)

    pair = jnp.arange(8, dtype=jnp.int32)
    carry = jnp.where(a >= b // 2, 0, -1)
    slots = (carry + pair // 2 - b % 2 - 2 * (pair % 2) + 8) % 4
    kernel_tiles = tiles(slots, orb, screen)

    level = lax.dynamic_index_in_dim(energies, place[a + 8 * (b // 4)], 0, keepdims=False)
    valence = lax.dynamic_slice_in_dim(level, (b % 4) * 8, 8, 0)
    gap = (level[None, NV:] - valence[:, None]).reshape(1, 256)
    return filtered(kpoints, kernel_tiles, column, own, gap)


def solution(mesh):
    placed = (P("row", "col", None), P(("row", "col"), None), P(), P(None, ("row", "col")), P())
    return jax.shard_map(
        per_device, mesh=mesh, in_specs=placed, out_specs=P(None, ("row", "col")), check_vma=False
    )
```

time: 1150 us -> 204 us (0.18)
  waiting for transfers between devices: 837 us -> 0 us
  Pallas kernels: 0 us -> 194 us
  local copies, waits for them, and re-layouts: 144 us -> 6.56 us
  matrix products: 106 us -> 0 us
  loops' own time: 31.5 us -> 0 us
  between operations: 13.7 us -> 2 us
    psum x3 -> x0, waiting for transfers between devices: 417 us -> none  [applied(): return lax.psum(apply_tiles(column_vectors), 'col')]
    all_gather x5 -> x0, waiting for transfers between devices: 397 us -> none  [the longest x1 214 us: per_device(): screen_all = lax.all_gather(screened, ('row', 'col'), axis=0, tiled=True)]
    pallas_call x0 -> x3, Pallas kernels: none -> 194 us  [the longest x1 102 us: filtered(): pl.pallas_call(filter_kernel, out_shape=jax.ShapeDtypeStruct((NX, 256), j...]
    dot_general x19 -> x0, matrix products: 106 us -> none  [the longest x8 55.8 us: pair_tile(): jnp.dot(amplitude, conduct.T, preferred_element_type=jnp.float32)]
    convert_element_type x10 -> x0, local copies, waits for them, and re-layouts: 92.1 us -> none  [the longest x8 90.6 us: pair_tile(): return inner_tile.reshape(NV * NC, NV * NC).astype(jnp.bfloat16)]
    another operation x1 -> x0, loops' own time: 31.5 us -> none  [per_device(): lax.map(build_tile, jnp.arange(row_points * col_points, dtype=jnp.int32))]
    all_to_all x2 -> x0, waiting for transfers between devices: 21.6 us -> none  [sent_to_all(): lax.all_to_all(jnp.broadcast_to(x[None], (length, *x.shape)), axis, 0, 0,...]
    dynamic_slice x23 -> x2, local copies, waits for them, and re-layouts: 20.8 us -> 0.6 us  [the longest x1 0.59 us: per_device(): place[a + 8 * (b // 4)]]
  transfers between devices with their start and end apart: 10 -> 0, of which waited for: 10 -> 0; matrix products, arithmetic and copies ran while one was open for 0% -> 0% of each run, Pallas kernels for 0% -> 0%
where the time goes in v1:
time: 204 us; the launch traced here: 203 us
  Pallas kernels  194 us (95%)
  local copies, waits for them, and re-layouts  6.56 us (3%)
    pallas_call x1, Pallas kernels, filtered(): pl.pallas_call(filter_kernel, out_shape=jax.ShapeDtypeStruct((NX, 256), j...  102 us
    pallas_call x1, Pallas kernels, gathered(): pl.pallas_call(gather_kernel, out_shape=(jax.ShapeDtypeStruct((6, 64, NG)...  72.6 us
    pallas_call x1, Pallas kernels, tiles(): pl.pallas_call(tile_kernel, out_shape=jax.ShapeDtypeStruct((16, 2 * PAIRS...  19.6 us
    unnamed x11, local copies, waits for them, and re-layouts  4.44 us

profile of v1, /device:TPU:0, one launch (start us, length us, event | category | flops | bytes accessed | tf_op | source)
XLA Modules:
  0.0 203.4 jit_solution(13774464188889256628)
XLA Ops:
  0.0 0.0 copy-start
  0.0 0.8 select_reduce_fusion.place
  0.8 0.6 dynamic_slice.10
  3.3 0.0 copy-done
  3.3 0.1 dynamic-slice_bitcast_fusion
  3.4 0.1 slice_bitcast_fusion
  3.5 0.1 broadcast_subtract_fusion
  3.6 0.6 sub.58.gap_ref
  4.2 0.7 reshape.35.orb_ref
  4.9 0.0 copy-start.2
  5.0 0.9 copy-done.2
  5.9 0.0 copy-start.4
  5.9 0.8 copy-done.4
  6.6 72.6 %gather.1 = (f32[6,64,512]{2,1,0:T(8,128)S(1)}, bf16[16,128,512]{2,1,0:T(8,128)(2,1)S(1)}, bf16[4,2,64,256]{3,2,1,0:T(8,128)(2,1)S(1)}, bf16[64,256]{1,0:T(8,128)(2,1)S(1)}) custom-call(s32[32]{0:T(128)S(1)} %select_reduce_fusion.place, bf16[4,16,128]{2,1,0:T(8,128)(2,1)S(1)} %reshape.35.orb_ref, bf16[128,512]{1,0:T(8,128)(2,1)S(1)} %copy-done.2, ...), custom_call_target="tpu_custom_call" | custom-call | tf_op jit(solution)/shard_map/gather/pallas_call | solution.py:206
  79.3 0.0 copy-start.1
  79.3 0.7 copy-done.1
  80.0 0.0 copy-start.3
  80.0 0.6 copy-done.3
  80.6 19.6 %tiles.1.kern_ref = bf16[16,2048,256]{2,1,0:T(8,128)(2,1)} custom-call(s32[8]{0:T(128)S(1)} %and_select_fusion.slots, f32[6,64,512]{2,1,0:T(8,128)S(1)} %get-tuple-element.9.orb_left.orb_right, f32[6,64,512]{2,1,0:T(8,128)S(1)} %get-tuple-element.9.orb_left.orb_right, bf16[4,512,512]{2,1,0:T(8,128)(2,1)S(1)} %bitcast.6), custom_call_target="tpu_custom_call" | custom-call | tf_op jit(solution)/shard_map/tiles/pallas_call | solution.py:286
  100.2 101.7 %filter.1 = f32[64,256]{1,0:T(8,128)} custom-call(s32[32]{0:T(128)} %value.1, bf16[16,2048,256]{2,1,0:T(8,128)(2,1)} %tiles.1.kern_ref, bf16[4,2,64,256]{3,2,1,0:T(8,128)(2,1)} %copy-done.1, bf16[64,256]{1,0:T(8,128)(2,1)} %copy-done.3, f32[1,256]{1,0:T(1,128)} %sub.58.gap_ref), custom_call_target="tpu_custom_call" | custom-call | tf_op jit(solution)/shard_map/filter/pallas_call | solution.py:487
  201.9 1.5 copy.7
  (2 shorter events, 0.0 us)
Async XLA Ops:
  0.0 3.3 %copy-start = (f32[32,64]{1,0:T(8,128)S(1)}, f32[32,64]{1,0:T(8,128)}, u32[]{:S(2)}) copy-start(f32[32,64]{1,0:T(8,128)} %param.9) | copy-start | bytes 24580
  4.9 0.9 copy-start.2
  5.9 0.8 copy-start.4
  79.3 0.7 copy-start.1
  80.0 0.6 copy-start.3

commit v2 on v0

v2 whole, which is shorter than its diff:
```python
import jax
import jax.numpy as jnp
from jax import lax
from jax.experimental import pallas as pl
from jax.experimental.pallas import tpu as pltpu
from jax.sharding import PartitionSpec as P

NV = 32
NC = 32
NG = 512
NX = 64
NK = 32
PAIRS = NV * NC
ROWS = 8
COLS = 16
SPREAD = 4.0
QUART = PAIRS // 4


def column_value(col, t):
    return col // 2 + 8 * lax.rem(col, 2) + 16 * t


def remote(src, dst, send_sem, recv_sem, row, col):
    return pltpu.make_async_remote_copy(
        src_ref=src,
        dst_ref=dst,
        send_sem=send_sem,
        recv_sem=recv_sem,
        device_id=(row, col),
        device_id_type=pl.DeviceIdType.MESH,
    )


def kernel(
    value,
    energy,
    orb_ref,
    screen_ref,
    vec_ref,
    out_ref,
    place,
    wide,
    orb_mine,
    orb_all,
    staged,
    landed,
    orb,
    screen,
    valence,
    conduct,
    amplitude,
    product,
    tiles,
    swap,
    vec_row,
    vec_sent,
    vec_got,
    own,
    gap,
    passed,
    column,
    ordered,
    sent,
    got,
    rounded,
    state,
    final_row,
    final_sent,
    final_got,
    s1,
    r1,
    s2,
    r2,
    sw,
    rw,
    lw,
    sf,
    sva,
    rva,
    lva,
    svb,
    rvb,
    st,
    rt,
    lt,
    sg,
    rg,
    lg,
    sp,
    rp,
    sa,
    ra,
    sb,
    rb,
):
    a = lax.axis_index("row")
    b = lax.axis_index("col")
    quarter = lax.rem(b, 4)
    group = b // 4
    chip = b // 2
    core = lax.rem(b, 2)
    level = a // 2

    for k in range(4):
        for part in range(4):
            wide[pl.ds(k * 16 + part, 4, stride=4), :] = orb_ref[k, :, part * 128 : part * 128 + 128].astype(
                jnp.float32
            )
    for k in range(4):
        orb_mine[k] = wide[k * 16 : k * 16 + 16].astype(jnp.bfloat16)

    def first_copy(d):
        return remote(
            orb_mine, orb_all.at[pl.ds(4 * a, 4)], s1.at[d], r1.at[d], lax.rem(a + d + 1, ROWS), b
        )

    @pl.loop(0, ROWS - 1)
    def _(d):
        first_copy(d).start()

    orb_all[pl.ds(4 * a, 4)] = orb_mine[...]

    def vec_row_copy(d):
        col = lax.rem(b + 4 * (d + 1), COLS)
        return remote(vec_ref, vec_row.at[group], sva.at[d], rva.at[d], a, col)

    def vec_row_local():
        return pltpu.make_async_copy(vec_ref, vec_row.at[group], lva)

    @pl.loop(0, NK)
    def _(wanted):
        found = jnp.int32(0)
        for k in range(NK):
            found = jnp.where(value[k] == wanted, k, found)
        place[wanted] = found

    @pl.loop(0, ROWS - 1)
    def _(d):
        first_copy(d).wait()

    @pl.loop(0, COLS)
    def _(dest):
        for m in range(4):
            staged[dest, m] = orb_all[place[a + 8 * m]]
        for t in range(2):
            staged[dest, 4 + t] = orb_all[place[column_value(dest, t)]]

    def second_copy(d):
        col = lax.rem(b + d + 1, COLS)
        return remote(staged.at[col], landed.at[b], s2.at[d], r2.at[d], a, col)

    @pl.loop(0, COLS - 1)
    def _(d):
        second_copy(d).start()

    landed[b] = staged[b]

    residue = lax.rem(4 * lax.rem(a, 2) + group, 8)
    piece = level * 4 + quarter
    needed = lax.rem(a - chip + 8, 8)

    def screen_target(i):
        row = 2 * lax.rem(level - i // 2 + 4, 4) + lax.rem(i, 2)
        return row, 2 * lax.rem(row - residue + 8, 8) + core

    def screen_copy(i):
        row, col = screen_target(i)
        return remote(screen_ref, screen.at[piece], sw.at[i], rw.at[piece], row, col)

    def screen_local():
        return pltpu.make_async_copy(screen_ref, screen.at[piece], lw)

    def screen_self(i):
        row, col = screen_target(i)
        return jnp.logical_and(row == a, col == b)

    def forward_copy(p):
        return remote(screen.at[p], screen.at[p], sf.at[p], rw.at[p], a, b + 1 - 2 * core)

    @pl.loop(0, 8)
    def _(i):
        @pl.when(screen_self(i))
        def _():
            screen_local().start()

        @pl.when(jnp.logical_not(screen_self(i)))
        def _():
            screen_copy(i).start()

    for d in range(3):
        vec_row_copy(d).start()
    vec_row_local().start()

    def arrive(slot):
        for half in range(2):
            p = slot * 4 + core + 2 * half
            here = jnp.logical_and(needed == residue, p == piece)

            @pl.when(here)
            def _():
                screen_local().wait()

            @pl.when(jnp.logical_not(here))
            def _():
                remote(screen_ref, screen.at[p], sw.at[0], rw.at[p], lax.rem(a + 1, ROWS), b).wait_recv()

            forward_copy(p).start()

    def forwarded(slot):
        for half in range(2):
            p = slot * 4 + 1 - core + 2 * half
            forward_copy(p).wait_recv()

    @pl.loop(0, 8)
    def _(i):
        row = lax.broadcasted_iota(jnp.int32, (128, PAIRS), 0) + i * 128
        col = lax.broadcasted_iota(jnp.int32, (128, PAIRS), 1)
        hit = jnp.logical_and((row & 31) == (col >> 5), (row >> 5) == (col & 31))
        swap[pl.ds(pl.multiple_of(i * 128, 128), 128)] = jnp.where(hit, 1.0, 0.0).astype(jnp.bfloat16)

    point = place[a + 8 * group]
    lane = lax.broadcasted_iota(jnp.int32, (8, QUART), 1)
    upper = jnp.zeros((8, QUART), jnp.float32)
    lower = jnp.zeros((8, QUART), jnp.float32)
    for c in range(NC):
        upper = jnp.where((lane & 31) == c, energy[point, NV + c], upper)
    for v in range(8):
        lower = jnp.where((lane >> 5) == v, energy[point, 8 * quarter + v], lower)
    gap[...] = upper - lower

    @pl.loop(0, COLS - 1)
    def _(d):
        second_copy(d).wait()

    @pl.loop(0, 6)
    def _(slot):
        for source in range(COLS):
            wide[source * 16 : source * 16 + 16] = landed[source, slot].astype(jnp.float32)
        for part in range(4):
            orb[slot, :, part * 128 : part * 128 + 128] = wide[pl.ds(part, 64, stride=4), :]

    def vec_cross_copy(d):
        return remote(
            vec_sent.at[d], vec_got.at[a], svb.at[d], rvb.at[d], lax.rem(a + d + 1, ROWS), b
        )

    def turn_copy(step, source):
        return remote(
            source, passed.at[step], st.at[step], rt.at[step], chip, 2 * a + core
        )

    def turn_local(step, source):
        return pltpu.make_async_copy(source, passed.at[step], lt.at[step])

    def turn_start(step, source):
        @pl.when(chip == a)
        def _():
            turn_local(step, source).start()

        @pl.when(chip != a)
        def _():
            turn_copy(step, source).start()

    part_index = (a // 4) * 4 + 2 * lax.rem(a, 2) + core
    spread_col = 2 * chip + lax.rem(a // 2, 2)

    def spread_self(i):
        return jnp.logical_and(i == 0, spread_col == b)

    def spread_copy(step, i):
        return remote(
            passed.at[step],
            column.at[step, part_index],
            sg.at[step, i],
            rg.at[step, part_index],
            lax.rem(a + i, ROWS),
            spread_col,
        )

    def spread_local(step, p):
        return pltpu.make_async_copy(passed.at[step], column.at[step, p], lg.at[step])

    def spread_start(step, source):
        @pl.when(chip == a)
        def _():
            turn_local(step, source).wait()

        @pl.when(chip != a)
        def _():
            turn_copy(step, source).wait()

        @pl.loop(0, ROWS)
        def _(i):
            @pl.when(spread_self(i))
            def _():
                spread_local(step, part_index).start()

            @pl.when(jnp.logical_not(spread_self(i)))
            def _():
                spread_copy(step, i).start()

    def spread_wait(step):
        @pl.loop(0, 8)
        def _(p):
            here = jnp.logical_and(spread_col == b, p == part_index)

            @pl.when(here)
            def _():
                spread_local(step, p).wait()

            @pl.when(jnp.logical_not(here))
            def _():
                remote(
                    passed.at[step],
                    column.at[step, p],
                    sg.at[step, 0],
                    rg.at[step, p],
                    lax.rem(a + 1, ROWS),
                    b,
                ).wait_recv()

    wrap = jnp.where(a >= chip, 0, 1)
    lane = lax.broadcasted_iota(jnp.int32, (32, 128), 1)
    low = lane < 64
    even = (lane & 32) == 0

    def build(slot, m, t):
        left, right = m, 4 + t
        for v in range(NV):
            valence[v * 32 : v * 32 + 32] = (orb[left, v : v + 1] * orb[right, :NV]).astype(jnp.bfloat16)
            conduct[v * 32 : v * 32 + 32] = (orb[right, NV + v : NV + v + 1] * orb[left, NV:]).astype(
                jnp.bfloat16
            )
        block = screen[pl.ds(slot * 4, 4)].reshape(NG, NG)
        amplitude[...] = jnp.dot(valence[...], block, preferred_element_type=jnp.float32).astype(jnp.bfloat16)
        for block in range(4):
            product[...] = lax.dot_general(
                amplitude[...],
                conduct[block * 256 : block * 256 + 256],
                (((1,), (1,)), ((), ())),
                preferred_element_type=jnp.float32,
            )
            for octet in range(8):
                for half in range(2):
                    s = [
                        product[octet * 128 + i * 32 : octet * 128 + i * 32 + 32, half * 128 : half * 128 + 128]
                        for i in range(4)
                    ]
                    u0 = jnp.where(low, s[0], pltpu.roll(s[2], 64, 1))
                    u2 = jnp.where(low, pltpu.roll(s[0], 64, 1), s[2])
                    u1 = jnp.where(low, s[1], pltpu.roll(s[3], 64, 1))
                    u3 = jnp.where(low, pltpu.roll(s[1], 64, 1), s[3])
                    turned = [
                        jnp.where(even, u0, pltpu.roll(u1, 32, 1)),
                        jnp.where(even, pltpu.roll(u0, 96, 1), u1),
                        jnp.where(even, u2, pltpu.roll(u3, 32, 1)),
                        jnp.where(even, pltpu.roll(u2, 96, 1), u3),
                    ]
                    first = block * 256 + half * 128
                    lanes = (octet % 2) * 128
                    for i in range(4):
                        tiles[m, octet // 2, t, first + i * 32 : first + i * 32 + 32, lanes : lanes + 128] = turned[
                            i
                        ].astype(jnp.bfloat16)

    arrive(level)

    @pl.loop(0, 4)
    def _(phase):
        slot = lax.rem(level + phase, 4)

        @pl.when(phase < 3)
        def _():
            arrive(lax.rem(slot + 1, 4))

        forwarded(slot)

        @pl.loop(0, 2)
        def _(t):
            build(slot, lax.rem(slot + wrap + core + 2 * t, 4), t)

        @pl.when(phase == 0)
        def _():
            for d in range(3):
                vec_row_copy(d).wait()
            vec_row_local().wait()
            for d in range(7):
                home = lax.rem(a + d + 1, ROWS) + 8 * group
                vec_sent[d] = vec_row[lax.rem(place[home], 4)]
                vec_cross_copy(d).start()
            vec_got[a] = vec_row[lax.rem(place[a + 8 * group], 4)]

        @pl.when(phase == 1)
        def _():
            for d in range(7):
                vec_cross_copy(d).wait()
            own[...] = vec_got[place[a + 8 * group] // 4]
            turn_start(0, own)

        @pl.when(phase == 2)
        def _():
            spread_start(0, own)

    @pl.loop(0, 8)
    def _(i):
        @pl.when(jnp.logical_not(screen_self(i)))
        def _():
            screen_copy(i).wait_send()

    for slot in range(4):
        for half in range(2):
            forward_copy(slot * 4 + core + 2 * half).wait_send()

    mine = own[...].astype(jnp.float32)
    levels = gap[0:1]

    def partial_copy(step, col):
        return remote(sent.at[step, col], got.at[step, b], sp.at[step, col], rp.at[step, b], a, col)

    def partial_arrival(step, source):
        return remote(sent.at[step, source], got.at[step, source], sp.at[step, source], rp.at[step, source], a, source)

    for step in range(3):
        spread_wait(step)
        for t in range(2):
            turned = jnp.zeros((NX, PAIRS), jnp.float32)
            for j in range(4):
                turned += jnp.dot(
                    column[step, t * 4 + j],
                    swap[j * QUART : j * QUART + QUART],
                    preferred_element_type=jnp.float32,
                )
            ordered[:, t * PAIRS : t * PAIRS + PAIRS] = turned.astype(jnp.bfloat16)

        @pl.loop(0, 4)
        def _(i):
            m = lax.rem(group + 1 + i, 4)
            for j in range(4):
                col = 4 * m + j
                sent[step, col] = jnp.dot(
                    ordered[...],
                    tiles[m, j].reshape(2 * PAIRS, QUART),
                    preferred_element_type=jnp.float32,
                ).astype(jnp.bfloat16)

                @pl.when(col != b)
                def _():
                    partial_copy(step, col).start()

        got[step, b] = sent[step, b]

        @pl.loop(0, COLS - 1)
        def _(d):
            source = lax.rem(b + d + 1, COLS)
            partial_arrival(step, source).wait_recv()

        total = jnp.zeros((NX, QUART), jnp.float32)
        for source in range(COLS):
            total += got[step, source].astype(jnp.float32)
        if step == 0:
            new = (levels * mine + total) / SPREAD
            state[0] = new
        elif step == 1:
            new = 2.0 * ((levels * state[0] + total) / SPREAD) - mine
            state[1] = new
        else:
            new = 2.0 * ((levels * state[1] + total) / SPREAD) - state[0]
        if step < 2:
            rounded[step] = new.astype(jnp.bfloat16)
            turn_start(step + 1, rounded.at[step])
            spread_start(step + 1, rounded.at[step])
        else:
            final_row[group] = new

    def row_copy(d):
        col = lax.rem(b + 4 * (d + 1), COLS)
        return remote(final_row.at[group], final_row.at[group], sa.at[d], ra.at[d], a, col)

    for d in range(3):
        row_copy(d).start()

    for step in range(3):

        @pl.loop(0, ROWS)
        def _(i):
            @pl.when(jnp.logical_not(spread_self(i)))
            def _():
                spread_copy(step, i).wait_send()

        @pl.loop(0, COLS - 1)
        def _(d):
            partial_copy(step, lax.rem(b + d + 1, COLS)).wait_send()

    for d in range(3):
        row_copy(d).wait()

    def last_copy(d):
        return remote(final_sent.at[d], final_got.at[a], sb.at[d], rb.at[d], lax.rem(a + d + 1, ROWS), b)

    for d in range(7):
        final_sent[d] = final_row[value[4 * lax.rem(a + d + 1, ROWS) + group] // 8]
        last_copy(d).start()
    final_got[a] = final_row[value[4 * a + group] // 8]
    for d in range(7):
        last_copy(d).wait()
    out_ref[...] = final_got[lax.rem(value[4 * a + group], 8)]


def per_device(orbitals, screened, kpoints, vectors, energies):
    dma = pltpu.SemaphoreType.DMA
    vmem = pl.BlockSpec(memory_space=pltpu.VMEM)
    smem = pl.BlockSpec(memory_space=pltpu.SMEM)
    anywhere = pl.BlockSpec(memory_space=pl.ANY)
    half, full = jnp.bfloat16, jnp.float32
    return pl.pallas_call(
        kernel,
        out_shape=jax.ShapeDtypeStruct((NX, QUART), full),
        in_specs=[smem, smem, vmem, anywhere, anywhere],
        out_specs=vmem,
        scratch_shapes=[
            pltpu.SMEM((NK,), jnp.int32),
            pltpu.VMEM((256, 128), full),
            pltpu.VMEM((4, 16, 128), half),
            pltpu.VMEM((NK, 16, 128), half),
            pltpu.VMEM((COLS, 6, 16, 128), half),
            pltpu.VMEM((COLS, 6, 16, 128), half),
            pltpu.VMEM((6, 64, NG), full),
            pltpu.VMEM((16, 128, NG), half),
            pltpu.VMEM((PAIRS, NG), half),
            pltpu.VMEM((PAIRS, NG), half),
            pltpu.VMEM((PAIRS, NG), half),
            pltpu.VMEM((PAIRS, 256), full),
            pltpu.VMEM((4, 4, 2, PAIRS, QUART), half),
            pltpu.VMEM((PAIRS, PAIRS), half),
            pltpu.VMEM((4, NX, QUART), half),
            pltpu.VMEM((7, NX, QUART), half),
            pltpu.VMEM((8, NX, QUART), half),
            pltpu.VMEM((NX, QUART), half),
            pltpu.VMEM((8, QUART), full),
            pltpu.VMEM((3, NX, QUART), half),
            pltpu.VMEM((3, 8, NX, QUART), half),
            pltpu.VMEM((NX, 2 * PAIRS), half),
            pltpu.VMEM((3, COLS, NX, QUART), half),
            pltpu.VMEM((3, COLS, NX, QUART), half),
            pltpu.VMEM((2, NX, QUART), half),
            pltpu.VMEM((2, NX, QUART), full),
            pltpu.VMEM((4, NX, QUART), full),
            pltpu.VMEM((7, NX, QUART), full),
            pltpu.VMEM((8, NX, QUART), full),
            dma((7,)),
            dma((7,)),
            dma((15,)),
            dma((15,)),
            dma((8,)),
            dma((16,)),
            dma,
            dma((16,)),
            dma((3,)),
            dma((3,)),
            dma,
            dma((7,)),
            dma((7,)),
            dma((3,)),
            dma((3,)),
            dma((3,)),
            dma((3, 8)),
            dma((3, 8)),
            dma((3,)),
            dma((3, 16)),
            dma((3, 16)),
            dma((3,)),
            dma((3,)),
            dma((7,)),
            dma((7,)),
        ],
        compiler_params=pltpu.CompilerParams(has_side_effects=True, vmem_limit_bytes=56 << 20),
        name="mega",
    )(kpoints, energies, orbitals, screened, vectors)


def solution(mesh):
    placed = (P("row", "col", None), P(("row", "col"), None), P(), P(None, ("row", "col")), P())
    return jax.shard_map(
        per_device, mesh=mesh, in_specs=placed, out_specs=P(None, ("row", "col")), check_vma=False
    )
```

time: 1150 us -> 133 us (0.12)
  waiting for transfers between devices: 837 us -> 0 us
  local copies, waits for them, and re-layouts: 144 us -> 1.47 us
  Pallas kernels: 0 us -> 130 us
  matrix products: 106 us -> 0 us
  loops' own time: 31.5 us -> 0 us
  between operations: 13.7 us -> 0.01 us
    psum x3 -> x0, waiting for transfers between devices: 417 us -> none  [applied(): return lax.psum(apply_tiles(column_vectors), 'col')]
    all_gather x5 -> x0, waiting for transfers between devices: 397 us -> none  [the longest x1 214 us: per_device(): screen_all = lax.all_gather(screened, ('row', 'col'), axis=0, tiled=True)]
    pallas_call x0 -> x1, Pallas kernels: none -> 130 us  [per_device(): pl.pallas_call(kernel, out_shape=jax.ShapeDtypeStruct((NX, QUART), full),...]
    dot_general x19 -> x0, matrix products: 106 us -> none  [the longest x8 55.8 us: pair_tile(): jnp.dot(amplitude, conduct.T, preferred_element_type=jnp.float32)]
    convert_element_type x10 -> x0, local copies, waits for them, and re-layouts: 92.1 us -> none  [the longest x8 90.6 us: pair_tile(): return inner_tile.reshape(NV * NC, NV * NC).astype(jnp.bfloat16)]
    another operation x1 -> x0, loops' own time: 31.5 us -> none  [per_device(): lax.map(build_tile, jnp.arange(row_points * col_points, dtype=jnp.int32))]
    all_to_all x2 -> x0, waiting for transfers between devices: 21.6 us -> none  [sent_to_all(): lax.all_to_all(jnp.broadcast_to(x[None], (length, *x.shape)), axis, 0, 0,...]
    dynamic_slice x23 -> x0, local copies, waits for them, and re-layouts: 20.8 us -> none  [the longest x8 11.2 us: build_tile(): right_point = kpoints[col_index * col_points + right_slot]]
  transfers between devices with their start and end apart: 10 -> 0, of which waited for: 10 -> 0; matrix products, arithmetic and copies ran while one was open for 0% -> 0% of each run, Pallas kernels for 0% -> 0%
where the time goes in v2:
time: 133 us; the launch traced here: 132 us
  Pallas kernels  130 us (98%)
  local copies, waits for them, and re-layouts  1.47 us (1%)
    pallas_call x1, Pallas kernels, per_device(): pl.pallas_call(kernel, out_shape=jax.ShapeDtypeStruct((NX, QUART), full),...  130 us

profile of v2, /device:TPU:0, one launch (start us, length us, event | category | flops | bytes accessed | tf_op | source)
XLA Modules:
  0.0 131.6 jit_solution(10857486354092262926)
XLA Ops:
  0.0 130.1 %mega.1 = f32[64,256]{1,0:T(8,128)} custom-call(s32[32]{0:T(128)} %value.1, f32[32,64]{1,0:T(8,128)} %energy.1, bf16[4,4,512]{2,1,0:T(4,128)(2,1)} %orb_ref.1, bf16[128,512]{1,0:T(8,128)(2,1)} %screen_ref.1, bf16[64,256]{1,0:T(8,128)(2,1)} %vec_ref.1), custom_call_target="tpu_custom_call" | custom-call | tf_op jit(solution)/shard_map/mega/pallas_call | solution.py:516
  130.1 1.5 %copy.7 = f32[64,256]{1,0:T(8,128)} copy(f32[64,256]{1,0:T(8,128)} %mega.1) | data formatting | bytes 131072

commit v3 on v2

--- a/solution.py
+++ b/solution.py
@@ -101,6 +101,45 @@
     chip = b // 2
     core = lax.rem(b, 2)
     level = a // 2
+    residue = lax.rem(4 * lax.rem(a, 2) + group, 8)
+    piece = level * 4 + quarter
+    needed = lax.rem(a - chip + 8, 8)
+
+    barrier = pltpu.get_barrier_semaphore()
+
+    def greet(row, col):
+        pl.semaphore_signal(barrier, inc=1, device_id=(row, col), device_id_type=pl.DeviceIdType.MESH)
+
+    @pl.loop(0, ROWS - 1)
+    def _(d):
+        greet(lax.rem(a + d + 1, ROWS), b)
+
+    @pl.loop(0, COLS - 1)
+    def _(d):
+        greet(a, lax.rem(b + d + 1, COLS))
+
+    @pl.loop(0, 8)
+    def _(i):
+        row = 2 * (i // 2) + needed // 4
+        col = 4 * lax.rem(needed, 4) + core + 2 * lax.rem(i, 2)
+
+        @pl.when(jnp.logical_or(row != a, col != b))
+        def _():
+            greet(row, col)
+
+    @pl.when(chip != a)
+    def _():
+        greet(chip, 2 * a + core)
+
+    @pl.loop(0, 4)
+    def _(i):
+        greet(2 * core + lax.rem(i, 2) + 4 * (i // 2), b + 1 - 2 * core)
+
+    peers = ROWS - 1 + COLS - 1 + 7
+    peers += jnp.where(needed != residue, 1, 0)
+    peers += jnp.where(chip != a, 1, 0)
+    peers += jnp.where(lax.rem(level, 2) != core, 8, 0)
+    pl.semaphore_wait(barrier, peers)
 
     for k in range(4):
         for part in range(4):
@@ -128,6 +167,34 @@
     def vec_row_local():
         return pltpu.make_async_copy(vec_ref, vec_row.at[group], lva)
 
+    def screen_target(i):
+        row = 2 * lax.rem(level - i // 2 + 4, 4) + lax.rem(i, 2)
+        return row, 2 * lax.rem(row - residue + 8, 8) + core
+
+    def screen_copy(i):
+        row, col = screen_target(i)
+        return remote(screen_ref, screen.at[piece], sw.at[i], rw.at[piece], row, col)
+
+    def screen_local():
+        return pltpu.make_async_copy(screen_ref, screen.at[piece], lw)
+
+    def screen_self(i):
+        row, col = screen_target(i)
+        return jnp.logical_and(row == a, col == b)
+
+    def forward_copy(p):
+        return remote(screen.at[p], screen.at[p], sf.at[p], rw.at[p], a, b + 1 - 2 * core)
+
+    @pl.loop(0, 8)
+    def _(i):
+        @pl.when(screen_self(i))
+        def _():
+            screen_local().start()
+
+        @pl.when(jnp.logical_not(screen_self(i)))
+        def _():
+            screen_copy(i).start()
+
     @pl.loop(0, NK)
     def _(wanted):
         found = jnp.int32(0)
@@ -155,38 +222,6 @@
         second_copy(d).start()
 
     landed[b] = staged[b]
-
-    residue = lax.rem(4 * lax.rem(a, 2) + group, 8)
-    piece = level * 4 + quarter
-    needed = lax.rem(a - chip + 8, 8)
-
-    def screen_target(i):
-        row = 2 * lax.rem(level - i // 2 + 4, 4) + lax.rem(i, 2)
-        return row, 2 * lax.rem(row - residue + 8, 8) + core
-
-    def screen_copy(i):
-        row, col = screen_target(i)
-        return remote(screen_ref, screen.at[piece], sw.at[i], rw.at[piece], row, col)
-
-    def screen_local():
-        return pltpu.make_async_copy(screen_ref, screen.at[piece], lw)
-
-    def screen_self(i):
-        row, col = screen_target(i)
-        return jnp.logical_and(row == a, col == b)
-
-    def forward_copy(p):
-        return remote(screen.at[p], screen.at[p], sf.at[p], rw.at[p], a, b + 1 - 2 * core)
-
-    @pl.loop(0, 8)
-    def _(i):
-        @pl.when(screen_self(i))
-        def _():
-            screen_local().start()
-
-        @pl.when(jnp.logical_not(screen_self(i)))
-        def _():
-            screen_copy(i).start()
 
     for d in range(3):
         vec_row_copy(d).start()
@@ -471,7 +506,7 @@
             turn_start(step + 1, rounded.at[step])
             spread_start(step + 1, rounded.at[step])
         else:
-            final_row[group] = new
+            final_row[group] = new.astype(jnp.bfloat16)
 
     def row_copy(d):
         col = lax.rem(b + 4 * (d + 1), COLS)
@@ -504,7 +539,7 @@
     final_got[a] = final_row[value[4 * a + group] // 8]
     for d in range(7):
         last_copy(d).wait()
-    out_ref[...] = final_got[lax.rem(value[4 * a + group], 8)]
+    out_ref[...] = final_got[lax.rem(value[4 * a + group], 8)].astype(jnp.float32)
 
 
 def per_device(orbitals, screened, kpoints, vectors, energies):
@@ -545,9 +580,9 @@
             pltpu.VMEM((3, COLS, NX, QUART), half),
             pltpu.VMEM((2, NX, QUART), half),
             pltpu.VMEM((2, NX, QUART), full),
-            pltpu.VMEM((4, NX, QUART), full),
-            pltpu.VMEM((7, NX, QUART), full),
-            pltpu.VMEM((8, NX, QUART), full),
+            pltpu.VMEM((4, NX, QUART), half),
+            pltpu.VMEM((7, NX, QUART), half),
+            pltpu.VMEM((8, NX, QUART), half),
             dma((7,)),
             dma((7,)),
             dma((15,)),
@@ -574,7 +609,8 @@
             dma((7,)),
             dma((7,)),
         ],
-        compiler_params=pltpu.CompilerParams(has_side_effects=True, vmem_limit_bytes=56 << 20),
+        compiler_params=pltpu.CompilerParams(
+            has_side_effects=True, collective_id=0, vmem_limit_bytes=56 << 20),
         name="mega",
     )(kpoints, energies, orbitals, screened, vectors)
 

time: 133 us -> 124 us (0.932)
  Pallas kernels: 130 us -> 121 us
    pallas_call x1, Pallas kernels: 130 us -> 121 us  [per_device(): pl.pallas_call(kernel, out_shape=jax.ShapeDtypeStruct((NX, QUART), full),...]
where the time goes in v3:
time: 124 us; the launch traced here: 123 us
  Pallas kernels  121 us (98%)
  local copies, waits for them, and re-layouts  1.47 us (1%)
    pallas_call x1, Pallas kernels, per_device(): pl.pallas_call(kernel, out_shape=jax.ShapeDtypeStruct((NX, QUART), full),...  121 us

profile of v3, /device:TPU:0, one launch (start us, length us, event | category | flops | bytes accessed | tf_op | source)
XLA Modules:
  0.0 122.7 jit_solution(18007521346454090285)
XLA Ops:
  0.0 121.2 %mega.1 = f32[64,256]{1,0:T(8,128)} custom-call(s32[32]{0:T(128)} %value.1, f32[32,64]{1,0:T(8,128)} %energy.1, bf16[4,4,512]{2,1,0:T(4,128)(2,1)} %orb_ref.1, bf16[128,512]{1,0:T(8,128)(2,1)} %screen_ref.1, bf16[64,256]{1,0:T(8,128)(2,1)} %vec_ref.1), custom_call_target="tpu_custom_call" | custom-call | tf_op jit(solution)/shard_map/mega/pallas_call | solution.py:551
  121.2 1.5 %copy.7 = f32[64,256]{1,0:T(8,128)} copy(f32[64,256]{1,0:T(8,128)} %mega.1) | data formatting | bytes 131072

commit v4 on v3

--- a/solution.py
+++ b/solution.py
@@ -17,8 +17,29 @@
 QUART = PAIRS // 4
 
 
-def column_value(col, t):
-    return col // 2 + 8 * lax.rem(col, 2) + 16 * t
+def labels(row, col):
+    x, y, z = lax.rem(col, 8) // 2, 2 * (col // 8) + lax.rem(row, 2), row // 2
+    alpha = 4 * (z // 2) + 2 * lax.rem((y + 1) // 2, 2) + x // 2
+    beta = 4 * lax.rem((z + 1) // 2, 2) + 2 * (y // 2) + lax.rem((x + 1) // 2, 2)
+    return alpha, beta
+
+
+def device(alpha, beta, core):
+    ax, ay, az = lax.rem(alpha, 2), lax.rem(alpha // 2, 2), alpha // 4
+    bx, by, bz = lax.rem(beta, 2), lax.rem(beta // 2, 2), beta // 4
+    x = bx + ax * (3 - 2 * bx)
+    y = ay + by * (3 - 2 * ay)
+    z = bz + az * (3 - 2 * bz)
+    return 2 * z + lax.rem(y, 2), 8 * (y // 2) + 2 * x + core
+
+
+def order_of(beta):
+    return 4 * lax.rem(beta // 2, 2) + 2 * (beta // 4) + lax.rem(beta // 4 + beta, 2)
+
+
+def beta_of(order):
+    high = lax.rem(order // 2, 2)
+    return 4 * high + 2 * (order // 4) + lax.rem(order + high, 2)
 
 
 def remote(src, dst, send_sem, recv_sem, row, col):
@@ -83,7 +104,6 @@
     rvb,
     st,
     rt,
-    lt,
     sg,
     rg,
     lg,
@@ -93,57 +113,43 @@
     ra,
     sb,
     rb,
+    lb,
 ):
     a = lax.axis_index("row")
     b = lax.axis_index("col")
-    quarter = lax.rem(b, 4)
-    group = b // 4
-    chip = b // 2
     core = lax.rem(b, 2)
+    alpha, beta = labels(a, b)
+    order = order_of(beta)
     level = a // 2
-    residue = lax.rem(4 * lax.rem(a, 2) + group, 8)
-    piece = level * 4 + quarter
-    needed = lax.rem(a - chip + 8, 8)
+    part = lax.rem(b, 4)
+    residue = 4 * lax.rem(a, 2) + b // 4
+    piece = level * 4 + part
+    needed = lax.rem(alpha - beta + 8, 8)
+    group = order // 2
+    quarter = 2 * lax.rem(order, 2) + core
+    point_value = alpha + 8 * group
+    me = 2 * order + core
+
+    def peer(index):
+        return device(alpha, beta_of(index // 2), lax.rem(index, 2))
 
     barrier = pltpu.get_barrier_semaphore()
 
-    def greet(row, col):
-        pl.semaphore_signal(barrier, inc=1, device_id=(row, col), device_id_type=pl.DeviceIdType.MESH)
-
-    @pl.loop(0, ROWS - 1)
+    @pl.loop(1, ROWS * COLS)
     def _(d):
-        greet(lax.rem(a + d + 1, ROWS), b)
-
-    @pl.loop(0, COLS - 1)
-    def _(d):
-        greet(a, lax.rem(b + d + 1, COLS))
-
-    @pl.loop(0, 8)
-    def _(i):
-        row = 2 * (i // 2) + needed // 4
-        col = 4 * lax.rem(needed, 4) + core + 2 * lax.rem(i, 2)
-
-        @pl.when(jnp.logical_or(row != a, col != b))
-        def _():
-            greet(row, col)
-
-    @pl.when(chip != a)
-    def _():
-        greet(chip, 2 * a + core)
-
-    @pl.loop(0, 4)
-    def _(i):
-        greet(2 * core + lax.rem(i, 2) + 4 * (i // 2), b + 1 - 2 * core)
-
-    peers = ROWS - 1 + COLS - 1 + 7
-    peers += jnp.where(needed != residue, 1, 0)
-    peers += jnp.where(chip != a, 1, 0)
-    peers += jnp.where(lax.rem(level, 2) != core, 8, 0)
-    pl.semaphore_wait(barrier, peers)
+        other = lax.rem(a * COLS + b + d, ROWS * COLS)
+        pl.semaphore_signal(
+            barrier,
+            inc=1,
+            device_id=(other // COLS, lax.rem(other, COLS)),
+            device_id_type=pl.DeviceIdType.MESH,
+        )
+
+    pl.semaphore_wait(barrier, ROWS * COLS - 1)
 
     for k in range(4):
-        for part in range(4):
-            wide[pl.ds(k * 16 + part, 4, stride=4), :] = orb_ref[k, :, part * 128 : part * 128 + 128].astype(
+        for lanes in range(4):
+            wide[pl.ds(k * 16 + lanes, 4, stride=4), :] = orb_ref[k, :, lanes * 128 : lanes * 128 + 128].astype(
                 jnp.float32
             )
     for k in range(4):
@@ -160,16 +166,17 @@
 
     orb_all[pl.ds(4 * a, 4)] = orb_mine[...]
 
-    def vec_row_copy(d):
-        col = lax.rem(b + 4 * (d + 1), COLS)
-        return remote(vec_ref, vec_row.at[group], sva.at[d], rva.at[d], a, col)
-
-    def vec_row_local():
-        return pltpu.make_async_copy(vec_ref, vec_row.at[group], lva)
-
-    def screen_target(i):
-        row = 2 * lax.rem(level - i // 2 + 4, 4) + lax.rem(i, 2)
-        return row, 2 * lax.rem(row - residue + 8, 8) + core
+    vec_self = b // 2 == order
+
+    def vec_first_copy(label):
+        row, col = device(label, beta_of(b // 2), core)
+        return remote(vec_ref, vec_got.at[a], sva.at[label], rva.at[a], row, col)
+
+    def vec_first_local():
+        return pltpu.make_async_copy(vec_ref, vec_got.at[a], lva)
+
+    def screen_target(label):
+        return device(label, lax.rem(label - residue + 8, 8), core)
 
     def screen_copy(i):
         row, col = screen_target(i)
@@ -185,15 +192,18 @@
     def forward_copy(p):
         return remote(screen.at[p], screen.at[p], sf.at[p], rw.at[p], a, b + 1 - 2 * core)
 
-    @pl.loop(0, 8)
+    @pl.loop(0, 32)
     def _(i):
-        @pl.when(screen_self(i))
+        label = lax.rem(i + alpha, 8)
+        turn = lax.rem(level - screen_target(label)[0] // 2 + 4, 4) == i // 8
+
+        @pl.when(jnp.logical_and(turn, screen_self(label)))
         def _():
             screen_local().start()
 
-        @pl.when(jnp.logical_not(screen_self(i)))
-        def _():
-            screen_copy(i).start()
+        @pl.when(jnp.logical_and(turn, jnp.logical_not(screen_self(label))))
+        def _():
+            screen_copy(label).start()
 
     @pl.loop(0, NK)
     def _(wanted):
@@ -206,16 +216,21 @@
     def _(d):
         first_copy(d).wait()
 
+    def second_target(col):
+        return jnp.where(col // 8 == b // 8, a, a + 1 - 2 * lax.rem(a, 2)), col
+
     @pl.loop(0, COLS)
     def _(dest):
+        row, col = second_target(dest)
+        alpha_there, beta_there = labels(row, col)
         for m in range(4):
-            staged[dest, m] = orb_all[place[a + 8 * m]]
+            staged[dest, m] = orb_all[place[alpha_there + 8 * m]]
         for t in range(2):
-            staged[dest, 4 + t] = orb_all[place[column_value(dest, t)]]
+            staged[dest, 4 + t] = orb_all[place[beta_there + 8 * lax.rem(col, 2) + 16 * t]]
 
     def second_copy(d):
-        col = lax.rem(b + d + 1, COLS)
-        return remote(staged.at[col], landed.at[b], s2.at[d], r2.at[d], a, col)
+        row, col = second_target(lax.rem(b + d + 1, COLS))
+        return remote(staged.at[col], landed.at[b], s2.at[d], r2.at[d], row, col)
 
     @pl.loop(0, COLS - 1)
     def _(d):
@@ -223,9 +238,19 @@
 
     landed[b] = staged[b]
 
-    for d in range(3):
-        vec_row_copy(d).start()
-    vec_row_local().start()
+    def vec_start():
+        @pl.loop(0, 8)
+        def _(i):
+            label = lax.rem(i + alpha, 8)
+            here = jnp.logical_and(vec_self, label == alpha)
+
+            @pl.when(here)
+            def _():
+                vec_first_local().start()
+
+            @pl.when(jnp.logical_not(here))
+            def _():
+                vec_first_copy(label).start()
 
     def arrive(slot):
         for half in range(2):
@@ -254,7 +279,7 @@
         hit = jnp.logical_and((row & 31) == (col >> 5), (row >> 5) == (col & 31))
         swap[pl.ds(pl.multiple_of(i * 128, 128), 128)] = jnp.where(hit, 1.0, 0.0).astype(jnp.bfloat16)
 
-    point = place[a + 8 * group]
+    point = place[point_value]
     lane = lax.broadcasted_iota(jnp.int32, (8, QUART), 1)
     upper = jnp.zeros((8, QUART), jnp.float32)
     lower = jnp.zeros((8, QUART), jnp.float32)
@@ -272,58 +297,44 @@
     def _(slot):
         for source in range(COLS):
             wide[source * 16 : source * 16 + 16] = landed[source, slot].astype(jnp.float32)
-        for part in range(4):
-            orb[slot, :, part * 128 : part * 128 + 128] = wide[pl.ds(part, 64, stride=4), :]
-
-    def vec_cross_copy(d):
-        return remote(
-            vec_sent.at[d], vec_got.at[a], svb.at[d], rvb.at[d], lax.rem(a + d + 1, ROWS), b
-        )
+        for lanes in range(4):
+            orb[slot, :, lanes * 128 : lanes * 128 + 128] = wide[pl.ds(lanes, 64, stride=4), :]
+
+    def vec_second_copy(d):
+        index = lax.rem(me + 4 * (d + 1), COLS)
+        row, col = peer(index)
+        return remote(vec_sent.at[d], vec_row.at[group], svb.at[d], rvb.at[d], row, col)
 
     def turn_copy(step, source):
-        return remote(
-            source, passed.at[step], st.at[step], rt.at[step], chip, 2 * a + core
-        )
-
-    def turn_local(step, source):
-        return pltpu.make_async_copy(source, passed.at[step], lt.at[step])
-
-    def turn_start(step, source):
-        @pl.when(chip == a)
-        def _():
-            turn_local(step, source).start()
-
-        @pl.when(chip != a)
-        def _():
-            turn_copy(step, source).start()
-
-    part_index = (a // 4) * 4 + 2 * lax.rem(a, 2) + core
-    spread_col = 2 * chip + lax.rem(a // 2, 2)
+        row, col = device(7 - beta, alpha, core)
+        return remote(source, passed.at[step], st.at[step], rt.at[step], row, col)
+
+    turned_order = order_of(7 - alpha)
+    part_index = (turned_order // 4) * 4 + 2 * lax.rem(turned_order, 2) + core
+    spread_core = lax.rem(turned_order // 2, 2)
+
+    def spread_target(i):
+        return device(lax.rem(alpha + i, 8), beta, spread_core)
 
     def spread_self(i):
-        return jnp.logical_and(i == 0, spread_col == b)
+        return jnp.logical_and(i == 0, spread_core == core)
 
     def spread_copy(step, i):
+        row, col = spread_target(i)
         return remote(
             passed.at[step],
             column.at[step, part_index],
             sg.at[step, i],
             rg.at[step, part_index],
-            lax.rem(a + i, ROWS),
-            spread_col,
+            row,
+            col,
         )
 
     def spread_local(step, p):
         return pltpu.make_async_copy(passed.at[step], column.at[step, p], lg.at[step])
 
     def spread_start(step, source):
-        @pl.when(chip == a)
-        def _():
-            turn_local(step, source).wait()
-
-        @pl.when(chip != a)
-        def _():
-            turn_copy(step, source).wait()
+        turn_copy(step, source).wait()
 
         @pl.loop(0, ROWS)
         def _(i):
@@ -338,7 +349,7 @@
     def spread_wait(step):
         @pl.loop(0, 8)
         def _(p):
-            here = jnp.logical_and(spread_col == b, p == part_index)
+            here = jnp.logical_and(spread_core == core, p == part_index)
 
             @pl.when(here)
             def _():
@@ -355,7 +366,7 @@
                     b,
                 ).wait_recv()
 
-    wrap = jnp.where(a >= chip, 0, 1)
+    wrap = jnp.where(alpha >= beta, 0, 1)
     lane = lax.broadcasted_iota(jnp.int32, (32, 128), 1)
     low = lane < 64
     even = (lane & 32) == 0
@@ -417,25 +428,46 @@
 
         @pl.when(phase == 0)
         def _():
+            vec_start()
+
+        @pl.when(phase == 1)
+        def _():
+            @pl.loop(0, 8)
+            def _(i):
+                here = jnp.logical_and(vec_self, i == alpha)
+
+                @pl.when(jnp.logical_not(here))
+                def _():
+                    vec_first_copy(i).wait_send()
+
+            @pl.loop(0, 8)
+            def _(i):
+                here = jnp.logical_and(vec_self, i == a)
+
+                @pl.when(here)
+                def _():
+                    vec_first_local().wait()
+
+                @pl.when(jnp.logical_not(here))
+                def _():
+                    remote(
+                        vec_ref, vec_got.at[i], sva.at[0], rva.at[i], lax.rem(a + 1, ROWS), b
+                    ).wait_recv()
+
             for d in range(3):
-                vec_row_copy(d).wait()
-            vec_row_local().wait()
-            for d in range(7):
-                home = lax.rem(a + d + 1, ROWS) + 8 * group
-                vec_sent[d] = vec_row[lax.rem(place[home], 4)]
-                vec_cross_copy(d).start()
-            vec_got[a] = vec_row[lax.rem(place[a + 8 * group], 4)]
-
-        @pl.when(phase == 1)
-        def _():
-            for d in range(7):
-                vec_cross_copy(d).wait()
-            own[...] = vec_got[place[a + 8 * group] // 4]
-            turn_start(0, own)
+                home = alpha + 8 * lax.rem(group + d + 1, 4)
+                vec_sent[d] = vec_got[place[home] // 4]
+                vec_second_copy(d).start()
+            vec_row[group] = vec_got[place[point_value] // 4]
 
         @pl.when(phase == 2)
         def _():
-            spread_start(0, own)
+            for d in range(3):
+                vec_second_copy(d).wait()
+            own[...] = vec_row[lax.rem(place[point_value], 4)]
+            turn_copy(0, own).start()
+
+    spread_start(0, own)
 
     @pl.loop(0, 8)
     def _(i):
@@ -450,11 +482,13 @@
     mine = own[...].astype(jnp.float32)
     levels = gap[0:1]
 
-    def partial_copy(step, col):
-        return remote(sent.at[step, col], got.at[step, b], sp.at[step, col], rp.at[step, b], a, col)
-
-    def partial_arrival(step, source):
-        return remote(sent.at[step, source], got.at[step, source], sp.at[step, source], rp.at[step, source], a, source)
+    def partial_copy(step, index):
+        row, col = peer(index)
+        return remote(sent.at[step, index], got.at[step, me], sp.at[step, index], rp.at[step, me], row, col)
+
+    def partial_arrival(step, index):
+        row, col = peer(index)
+        return remote(sent.at[step, index], got.at[step, index], sp.at[step, index], rp.at[step, index], row, col)
 
     for step in range(3):
         spread_wait(step)
@@ -472,23 +506,22 @@
         def _(i):
             m = lax.rem(group + 1 + i, 4)
             for j in range(4):
-                col = 4 * m + j
-                sent[step, col] = jnp.dot(
+                index = 4 * m + j
+                sent[step, index] = jnp.dot(
                     ordered[...],
                     tiles[m, j].reshape(2 * PAIRS, QUART),
                     preferred_element_type=jnp.float32,
                 ).astype(jnp.bfloat16)
 
-                @pl.when(col != b)
+                @pl.when(index != me)
                 def _():
-                    partial_copy(step, col).start()
-
-        got[step, b] = sent[step, b]
+                    partial_copy(step, index).start()
+
+        got[step, me] = sent[step, me]
 
         @pl.loop(0, COLS - 1)
         def _(d):
-            source = lax.rem(b + d + 1, COLS)
-            partial_arrival(step, source).wait_recv()
+            partial_arrival(step, lax.rem(me + d + 1, COLS)).wait_recv()
 
         total = jnp.zeros((NX, QUART), jnp.float32)
         for source in range(COLS):
@@ -503,14 +536,14 @@
             new = 2.0 * ((levels * state[1] + total) / SPREAD) - state[0]
         if step < 2:
             rounded[step] = new.astype(jnp.bfloat16)
-            turn_start(step + 1, rounded.at[step])
+            turn_copy(step + 1, rounded.at[step]).start()
             spread_start(step + 1, rounded.at[step])
         else:
             final_row[group] = new.astype(jnp.bfloat16)
 
     def row_copy(d):
-        col = lax.rem(b + 4 * (d + 1), COLS)
-        return remote(final_row.at[group], final_row.at[group], sa.at[d], ra.at[d], a, col)
+        row, col = peer(lax.rem(me + 4 * (d + 1), COLS))
+        return remote(final_row.at[group], final_row.at[group], sa.at[d], ra.at[d], row, col)
 
     for d in range(3):
         row_copy(d).start()
@@ -525,21 +558,50 @@
 
         @pl.loop(0, COLS - 1)
         def _(d):
-            partial_copy(step, lax.rem(b + d + 1, COLS)).wait_send()
+            partial_copy(step, lax.rem(me + d + 1, COLS)).wait_send()
 
     for d in range(3):
         row_copy(d).wait()
 
-    def last_copy(d):
-        return remote(final_sent.at[d], final_got.at[a], sb.at[d], rb.at[d], lax.rem(a + d + 1, ROWS), b)
-
-    for d in range(7):
-        final_sent[d] = final_row[value[4 * lax.rem(a + d + 1, ROWS) + group] // 8]
-        last_copy(d).start()
-    final_got[a] = final_row[value[4 * a + group] // 8]
-    for d in range(7):
-        last_copy(d).wait()
-    out_ref[...] = final_got[lax.rem(value[4 * a + group], 8)].astype(jnp.float32)
+    def last_copy(i):
+        row = lax.rem(a + i, ROWS)
+        return remote(final_sent.at[i], final_got.at[alpha], sb.at[i], rb.at[alpha], row, me)
+
+    def last_self(i):
+        return jnp.logical_and(i == 0, me == b)
+
+    for i in range(ROWS):
+        final_sent[i] = final_row[value[4 * lax.rem(a + i, ROWS) + group] // 8]
+
+        @pl.when(jnp.logical_not(last_self(i)))
+        def _():
+            last_copy(i).start()
+
+        @pl.when(last_self(i))
+        def _():
+            pltpu.make_async_copy(final_sent.at[i], final_got.at[alpha], lb).start()
+
+    @pl.loop(0, 8)
+    def _(label):
+        here = jnp.logical_and(me == b, label == alpha)
+
+        @pl.when(here)
+        def _():
+            pltpu.make_async_copy(final_sent.at[0], final_got.at[label], lb).wait()
+
+        @pl.when(jnp.logical_not(here))
+        def _():
+            remote(
+                final_sent.at[0], final_got.at[label], sb.at[0], rb.at[label], lax.rem(a + 1, ROWS), b
+            ).wait_recv()
+
+    out_ref[...] = final_got[lax.rem(value[4 * a + b // 4], 8)].astype(jnp.float32)
+
+    @pl.loop(0, ROWS)
+    def _(i):
+        @pl.when(jnp.logical_not(last_self(i)))
+        def _():
+            last_copy(i).wait_send()
 
 
 def per_device(orbitals, screened, kpoints, vectors, energies):
@@ -581,7 +643,7 @@
             pltpu.VMEM((2, NX, QUART), half),
             pltpu.VMEM((2, NX, QUART), full),
             pltpu.VMEM((4, NX, QUART), half),
-            pltpu.VMEM((7, NX, QUART), half),
+            pltpu.VMEM((8, NX, QUART), half),
             pltpu.VMEM((8, NX, QUART), half),
             dma((7,)),
             dma((7,)),
@@ -591,11 +653,10 @@
             dma((16,)),
             dma,
             dma((16,)),
+            dma((8,)),
+            dma((8,)),
+            dma,
             dma((3,)),
-            dma((3,)),
-            dma,
-            dma((7,)),
-            dma((7,)),
             dma((3,)),
             dma((3,)),
             dma((3,)),
@@ -606,8 +667,9 @@
             dma((3, 16)),
             dma((3,)),
             dma((3,)),
-            dma((7,)),
-            dma((7,)),
+            dma((8,)),
+            dma((8,)),
+            dma,
         ],
         compiler_params=pltpu.CompilerParams(
             has_side_effects=True, collective_id=0, vmem_limit_bytes=56 << 20),

time: 124 us -> 140 us (1.13)
  Pallas kernels: 121 us -> 138 us
    pallas_call x1, Pallas kernels: 121 us -> 138 us  [per_device(): pl.pallas_call(kernel, out_shape=jax.ShapeDtypeStruct((NX, QUART), full),...]
where the time goes in v4:
time: 140 us; the launch traced here: 139 us
  Pallas kernels  138 us (99%)
  local copies, waits for them, and re-layouts  1.47 us (1%)
    pallas_call x1, Pallas kernels, per_device(): pl.pallas_call(kernel, out_shape=jax.ShapeDtypeStruct((NX, QUART), full),...  138 us

profile of v4, /device:TPU:0, one launch (start us, length us, event | category | flops | bytes accessed | tf_op | source)
XLA Modules:
  0.0 139.4 jit_solution(14777480945230432525)
XLA Ops:
  0.0 137.9 %mega.1 = f32[64,256]{1,0:T(8,128)} custom-call(s32[32]{0:T(128)} %value.1, f32[32,64]{1,0:T(8,128)} %energy.1, bf16[4,4,512]{2,1,0:T(4,128)(2,1)} %orb_ref.1, bf16[128,512]{1,0:T(8,128)(2,1)} %screen_ref.1, bf16[64,256]{1,0:T(8,128)(2,1)} %vec_ref.1), custom_call_target="tpu_custom_call" | custom-call | tf_op jit(solution)/shard_map/mega/pallas_call | solution.py:613
  137.9 1.5 %copy.7 = f32[64,256]{1,0:T(8,128)} copy(f32[64,256]{1,0:T(8,128)} %mega.1) | data formatting | bytes 131072

commit v5 on v4

--- a/solution.py
+++ b/solution.py
@@ -15,31 +15,6 @@
 COLS = 16
 SPREAD = 4.0
 QUART = PAIRS // 4
-
-
-def labels(row, col):
-    x, y, z = lax.rem(col, 8) // 2, 2 * (col // 8) + lax.rem(row, 2), row // 2
-    alpha = 4 * (z // 2) + 2 * lax.rem((y + 1) // 2, 2) + x // 2
-    beta = 4 * lax.rem((z + 1) // 2, 2) + 2 * (y // 2) + lax.rem((x + 1) // 2, 2)
-    return alpha, beta
-
-
-def device(alpha, beta, core):
-    ax, ay, az = lax.rem(alpha, 2), lax.rem(alpha // 2, 2), alpha // 4
-    bx, by, bz = lax.rem(beta, 2), lax.rem(beta // 2, 2), beta // 4
-    x = bx + ax * (3 - 2 * bx)
-    y = ay + by * (3 - 2 * ay)
-    z = bz + az * (3 - 2 * bz)
-    return 2 * z + lax.rem(y, 2), 8 * (y // 2) + 2 * x + core
-
-
-def order_of(beta):
-    return 4 * lax.rem(beta // 2, 2) + 2 * (beta // 4) + lax.rem(beta // 4 + beta, 2)
-
-
-def beta_of(order):
-    high = lax.rem(order // 2, 2)
-    return 4 * high + 2 * (order // 4) + lax.rem(order + high, 2)
 
 
 def remote(src, dst, send_sem, recv_sem, row, col):
@@ -79,7 +54,6 @@
     vec_got,
     own,
     gap,
-    passed,
     column,
     ordered,
     sent,
@@ -102,8 +76,6 @@
     lva,
     svb,
     rvb,
-    st,
-    rt,
     sg,
     rg,
     lg,
@@ -118,34 +90,56 @@
     a = lax.axis_index("row")
     b = lax.axis_index("col")
     core = lax.rem(b, 2)
-    alpha, beta = labels(a, b)
-    order = order_of(beta)
+    alpha = b // 2
     level = a // 2
-    part = lax.rem(b, 4)
-    residue = 4 * lax.rem(a, 2) + b // 4
-    piece = level * 4 + part
-    needed = lax.rem(alpha - beta + 8, 8)
-    group = order // 2
-    quarter = 2 * lax.rem(order, 2) + core
-    point_value = alpha + 8 * group
-    me = 2 * order + core
-
-    def peer(index):
-        return device(alpha, beta_of(index // 2), lax.rem(index, 2))
+    side = lax.rem(a, 2)
+    residue = 4 * side + b // 4
+    piece = level * 4 + lax.rem(b, 4)
+    needed = lax.rem(alpha - a + 8, 8)
+    quarter = 2 * side + core
+    point_value = alpha + 8 * level
+    me = 2 * a + core
+    plane_self = lax.rem(alpha, 2) == side
+    spread_core = lax.rem(level, 2)
+    spread_own = jnp.logical_and(alpha == a, spread_core == core)
+
+    def plane_device(i):
+        return 2 * level + i // 4, 4 * lax.rem(i, 4) + quarter
+
+    def plane_owner(label):
+        return 2 * level + lax.rem(alpha, 2), 2 * label + core
 
     barrier = pltpu.get_barrier_semaphore()
 
-    @pl.loop(1, ROWS * COLS)
+    def greet(row, col):
+        pl.semaphore_signal(barrier, inc=1, device_id=(row, col), device_id_type=pl.DeviceIdType.MESH)
+
+    def greet_other(row, col):
+        @pl.when(jnp.logical_or(row != a, col != b))
+        def _():
+            greet(row, col)
+
+    @pl.loop(0, ROWS - 1)
     def _(d):
-        other = lax.rem(a * COLS + b + d, ROWS * COLS)
-        pl.semaphore_signal(
-            barrier,
-            inc=1,
-            device_id=(other // COLS, lax.rem(other, COLS)),
-            device_id_type=pl.DeviceIdType.MESH,
-        )
-
-    pl.semaphore_wait(barrier, ROWS * COLS - 1)
+        greet(lax.rem(a + d + 1, ROWS), b)
+        greet(lax.rem(a + d + 1, ROWS), b + 1 - 2 * core)
+
+    @pl.loop(0, COLS - 1)
+    def _(d):
+        greet(a, lax.rem(b + d + 1, COLS))
+
+    @pl.loop(0, 8)
+    def _(i):
+        greet_other(2 * (i // 2) + needed // 4, 4 * lax.rem(needed, 4) + core + 2 * lax.rem(i, 2))
+        greet_other(*plane_device(i))
+        greet_other(*plane_owner(i))
+        greet_other(4 * (i // 4) + 2 * core + lax.rem(i // 2, 2), 2 * a + lax.rem(i, 2))
+
+    peers = 2 * (ROWS - 1) + COLS - 1 + 32
+    peers -= jnp.where(needed == residue, 1, 0)
+    peers -= jnp.where(plane_self, 2, 0)
+    peers -= jnp.where(spread_own, 1, 0)
+    pl.semaphore_wait(barrier, peers)
 
     for k in range(4):
         for lanes in range(4):
@@ -166,17 +160,16 @@
 
     orb_all[pl.ds(4 * a, 4)] = orb_mine[...]
 
-    vec_self = b // 2 == order
-
     def vec_first_copy(label):
-        row, col = device(label, beta_of(b // 2), core)
-        return remote(vec_ref, vec_got.at[a], sva.at[label], rva.at[a], row, col)
+        row, col = plane_owner(label)
+        slot = 4 * side + b // 4
+        return remote(vec_ref, vec_got.at[slot], sva.at[label], rva.at[slot], row, col)
 
     def vec_first_local():
-        return pltpu.make_async_copy(vec_ref, vec_got.at[a], lva)
+        return pltpu.make_async_copy(vec_ref, vec_got.at[4 * side + b // 4], lva)
 
     def screen_target(label):
-        return device(label, lax.rem(label - residue + 8, 8), core)
+        return lax.rem(label - residue + 8, 8), 2 * label + core
 
     def screen_copy(i):
         row, col = screen_target(i)
@@ -216,21 +209,16 @@
     def _(d):
         first_copy(d).wait()
 
-    def second_target(col):
-        return jnp.where(col // 8 == b // 8, a, a + 1 - 2 * lax.rem(a, 2)), col
-
     @pl.loop(0, COLS)
     def _(dest):
-        row, col = second_target(dest)
-        alpha_there, beta_there = labels(row, col)
         for m in range(4):
-            staged[dest, m] = orb_all[place[alpha_there + 8 * m]]
+            staged[dest, m] = orb_all[place[dest // 2 + 8 * m]]
         for t in range(2):
-            staged[dest, 4 + t] = orb_all[place[beta_there + 8 * lax.rem(col, 2) + 16 * t]]
+            staged[dest, 4 + t] = orb_all[place[a + 8 * lax.rem(dest, 2) + 16 * t]]
 
     def second_copy(d):
-        row, col = second_target(lax.rem(b + d + 1, COLS))
-        return remote(staged.at[col], landed.at[b], s2.at[d], r2.at[d], row, col)
+        col = lax.rem(b + d + 1, COLS)
+        return remote(staged.at[col], landed.at[b], s2.at[d], r2.at[d], a, col)
 
     @pl.loop(0, COLS - 1)
     def _(d):
@@ -242,7 +230,7 @@
         @pl.loop(0, 8)
         def _(i):
             label = lax.rem(i + alpha, 8)
-            here = jnp.logical_and(vec_self, label == alpha)
+            here = jnp.logical_and(plane_self, label == alpha)
 
             @pl.when(here)
             def _():
@@ -301,64 +289,51 @@
             orb[slot, :, lanes * 128 : lanes * 128 + 128] = wide[pl.ds(lanes, 64, stride=4), :]
 
     def vec_second_copy(d):
-        index = lax.rem(me + 4 * (d + 1), COLS)
-        row, col = peer(index)
-        return remote(vec_sent.at[d], vec_row.at[group], svb.at[d], rvb.at[d], row, col)
-
-    def turn_copy(step, source):
-        row, col = device(7 - beta, alpha, core)
-        return remote(source, passed.at[step], st.at[step], rt.at[step], row, col)
-
-    turned_order = order_of(7 - alpha)
-    part_index = (turned_order // 4) * 4 + 2 * lax.rem(turned_order, 2) + core
-    spread_core = lax.rem(turned_order // 2, 2)
-
-    def spread_target(i):
-        return device(lax.rem(alpha + i, 8), beta, spread_core)
-
-    def spread_self(i):
-        return jnp.logical_and(i == 0, spread_core == core)
-
-    def spread_copy(step, i):
-        row, col = spread_target(i)
+        row = lax.rem(a + 2 * (d + 1), ROWS)
+        return remote(vec_sent.at[d], vec_row.at[level], svb.at[d], rvb.at[d], row, b)
+
+    part_index = (a // 4) * 4 + quarter
+
+    def spread_copy(step, source, i):
         return remote(
-            passed.at[step],
+            source,
             column.at[step, part_index],
             sg.at[step, i],
             rg.at[step, part_index],
-            row,
-            col,
+            alpha,
+            2 * lax.rem(alpha + i, 8) + spread_core,
         )
 
-    def spread_local(step, p):
-        return pltpu.make_async_copy(passed.at[step], column.at[step, p], lg.at[step])
+    def spread_local(step, source, p):
+        return pltpu.make_async_copy(source, column.at[step, p], lg.at[step])
+
+    def spread_self(i):
+        return jnp.logical_and(i == 0, spread_own)
 
     def spread_start(step, source):
-        turn_copy(step, source).wait()
-
         @pl.loop(0, ROWS)
         def _(i):
             @pl.when(spread_self(i))
             def _():
-                spread_local(step, part_index).start()
+                spread_local(step, source, part_index).start()
 
             @pl.when(jnp.logical_not(spread_self(i)))
             def _():
-                spread_copy(step, i).start()
-
-    def spread_wait(step):
+                spread_copy(step, source, i).start()
+
+    def spread_wait(step, source):
         @pl.loop(0, 8)
         def _(p):
-            here = jnp.logical_and(spread_core == core, p == part_index)
+            here = jnp.logical_and(spread_own, p == part_index)
 
             @pl.when(here)
             def _():
-                spread_local(step, p).wait()
+                spread_local(step, source, p).wait()
 
             @pl.when(jnp.logical_not(here))
             def _():
                 remote(
-                    passed.at[step],
+                    source,
                     column.at[step, p],
                     sg.at[step, 0],
                     rg.at[step, p],
@@ -366,7 +341,7 @@
                     b,
                 ).wait_recv()
 
-    wrap = jnp.where(alpha >= beta, 0, 1)
+    wrap = jnp.where(alpha >= a, 0, 1)
     lane = lax.broadcasted_iota(jnp.int32, (32, 128), 1)
     low = lane < 64
     even = (lane & 32) == 0
@@ -434,7 +409,7 @@
         def _():
             @pl.loop(0, 8)
             def _(i):
-                here = jnp.logical_and(vec_self, i == alpha)
+                here = jnp.logical_and(plane_self, i == alpha)
 
                 @pl.when(jnp.logical_not(here))
                 def _():
@@ -442,7 +417,7 @@
 
             @pl.loop(0, 8)
             def _(i):
-                here = jnp.logical_and(vec_self, i == a)
+                here = jnp.logical_and(plane_self, i == 4 * side + b // 4)
 
                 @pl.when(here)
                 def _():
@@ -455,19 +430,17 @@
                     ).wait_recv()
 
             for d in range(3):
-                home = alpha + 8 * lax.rem(group + d + 1, 4)
-                vec_sent[d] = vec_got[place[home] // 4]
+                home = alpha + 8 * lax.rem(level + d + 1, 4)
+                vec_sent[d] = vec_got[lax.rem(place[home], 8)]
                 vec_second_copy(d).start()
-            vec_row[group] = vec_got[place[point_value] // 4]
+            vec_row[level] = vec_got[lax.rem(place[point_value], 8)]
 
         @pl.when(phase == 2)
         def _():
             for d in range(3):
                 vec_second_copy(d).wait()
-            own[...] = vec_row[lax.rem(place[point_value], 4)]
-            turn_copy(0, own).start()
-
-    spread_start(0, own)
+            own[...] = vec_row[place[point_value] // 8]
+            spread_start(0, own)
 
     @pl.loop(0, 8)
     def _(i):
@@ -482,6 +455,9 @@
     mine = own[...].astype(jnp.float32)
     levels = gap[0:1]
 
+    def peer(index):
+        return index // 2, 2 * alpha + lax.rem(index, 2)
+
     def partial_copy(step, index):
         row, col = peer(index)
         return remote(sent.at[step, index], got.at[step, me], sp.at[step, index], rp.at[step, me], row, col)
@@ -491,7 +467,7 @@
         return remote(sent.at[step, index], got.at[step, index], sp.at[step, index], rp.at[step, index], row, col)
 
     for step in range(3):
-        spread_wait(step)
+        spread_wait(step, own if step == 0 else rounded.at[step - 1])
         for t in range(2):
             turned = jnp.zeros((NX, PAIRS), jnp.float32)
             for j in range(4):
@@ -504,7 +480,7 @@
 
         @pl.loop(0, 4)
         def _(i):
-            m = lax.rem(group + 1 + i, 4)
+            m = lax.rem(level + 1 + i, 4)
             for j in range(4):
                 index = 4 * m + j
                 sent[step, index] = jnp.dot(
@@ -536,14 +512,13 @@
             new = 2.0 * ((levels * state[1] + total) / SPREAD) - state[0]
         if step < 2:
             rounded[step] = new.astype(jnp.bfloat16)
-            turn_copy(step + 1, rounded.at[step]).start()
             spread_start(step + 1, rounded.at[step])
         else:
-            final_row[group] = new.astype(jnp.bfloat16)
+            final_row[level] = new.astype(jnp.bfloat16)
 
     def row_copy(d):
-        row, col = peer(lax.rem(me + 4 * (d + 1), COLS))
-        return remote(final_row.at[group], final_row.at[group], sa.at[d], ra.at[d], row, col)
+        row = lax.rem(a + 2 * (d + 1), ROWS)
+        return remote(final_row.at[level], final_row.at[level], sa.at[d], ra.at[d], row, b)
 
     for d in range(3):
         row_copy(d).start()
@@ -554,7 +529,7 @@
         def _(i):
             @pl.when(jnp.logical_not(spread_self(i)))
             def _():
-                spread_copy(step, i).wait_send()
+                spread_copy(step, own if step == 0 else rounded.at[step - 1], i).wait_send()
 
         @pl.loop(0, COLS - 1)
         def _(d):
@@ -564,14 +539,17 @@
         row_copy(d).wait()
 
     def last_copy(i):
-        row = lax.rem(a + i, ROWS)
-        return remote(final_sent.at[i], final_got.at[alpha], sb.at[i], rb.at[alpha], row, me)
+        row, col = plane_device(i)
+        return remote(final_sent.at[i], final_got.at[alpha], sb.at[i], rb.at[alpha], row, col)
+
+    def last_local(label):
+        return pltpu.make_async_copy(final_sent.at[4 * side + b // 4], final_got.at[label], lb)
 
     def last_self(i):
-        return jnp.logical_and(i == 0, me == b)
+        return jnp.logical_and(plane_self, i == 4 * side + b // 4)
 
     for i in range(ROWS):
-        final_sent[i] = final_row[value[4 * lax.rem(a + i, ROWS) + group] // 8]
+        final_sent[i] = final_row[value[8 * level + i] // 8]
 
         @pl.when(jnp.logical_not(last_self(i)))
         def _():
@@ -579,15 +557,15 @@
 
         @pl.when(last_self(i))
         def _():
-            pltpu.make_async_copy(final_sent.at[i], final_got.at[alpha], lb).start()
+            last_local(alpha).start()
 
     @pl.loop(0, 8)
     def _(label):
-        here = jnp.logical_and(me == b, label == alpha)
+        here = jnp.logical_and(plane_self, label == alpha)
 
         @pl.when(here)
         def _():
-            pltpu.make_async_copy(final_sent.at[0], final_got.at[label], lb).wait()
+            last_local(label).wait()
 
         @pl.when(jnp.logical_not(here))
         def _():
@@ -635,7 +613,6 @@
             pltpu.VMEM((8, NX, QUART), half),
             pltpu.VMEM((NX, QUART), half),
             pltpu.VMEM((8, QUART), full),
-            pltpu.VMEM((3, NX, QUART), half),
             pltpu.VMEM((3, 8, NX, QUART), half),
             pltpu.VMEM((NX, 2 * PAIRS), half),
             pltpu.VMEM((3, COLS, NX, QUART), half),
@@ -658,8 +635,6 @@
             dma,
             dma((3,)),
             dma((3,)),
-            dma((3,)),
-            dma((3,)),
             dma((3, 8)),
             dma((3, 8)),
             dma((3,)),

time: 140 us -> 119 us (0.85)
  Pallas kernels: 138 us -> 117 us
    pallas_call x1, Pallas kernels: 138 us -> 117 us  [per_device(): pl.pallas_call(kernel, out_shape=jax.ShapeDtypeStruct((NX, QUART), full),...]
where the time goes in v5:
time: 119 us; the launch traced here: 118 us
  Pallas kernels  117 us (98%)
  local copies, waits for them, and re-layouts  1.47 us (1%)
    pallas_call x1, Pallas kernels, per_device(): pl.pallas_call(kernel, out_shape=jax.ShapeDtypeStruct((NX, QUART), full),...  117 us

profile of v5, /device:TPU:0, one launch (start us, length us, event | category | flops | bytes accessed | tf_op | source)
XLA Modules:
  0.0 118.3 jit_solution(7348741927459314398)
XLA Ops:
  0.0 116.8 %mega.1 = f32[64,256]{1,0:T(8,128)} custom-call(s32[32]{0:T(128)} %value.1, f32[32,64]{1,0:T(8,128)} %energy.1, bf16[4,4,512]{2,1,0:T(4,128)(2,1)} %orb_ref.1, bf16[128,512]{1,0:T(8,128)(2,1)} %screen_ref.1, bf16[64,256]{1,0:T(8,128)(2,1)} %vec_ref.1), custom_call_target="tpu_custom_call" | custom-call | tf_op jit(solution)/shard_map/mega/pallas_call | solution.py:591
  116.8 1.5 %copy.7 = f32[64,256]{1,0:T(8,128)} copy(f32[64,256]{1,0:T(8,128)} %mega.1) | data formatting | bytes 131072

commit v6 on v5

--- a/solution.py
+++ b/solution.py
@@ -53,6 +53,7 @@
     vec_sent,
     vec_got,
     own,
+    own_swapped,
     gap,
     column,
     ordered,
@@ -73,19 +74,16 @@
     sf,
     sva,
     rva,
-    lva,
     svb,
     rvb,
     sg,
     rg,
-    lg,
     sp,
     rp,
     sa,
     ra,
     sb,
     rb,
-    lb,
 ):
     a = lax.axis_index("row")
     b = lax.axis_index("col")
@@ -139,8 +137,6 @@
     peers -= jnp.where(needed == residue, 1, 0)
     peers -= jnp.where(plane_self, 2, 0)
     peers -= jnp.where(spread_own, 1, 0)
-    pl.semaphore_wait(barrier, peers)
-
     for k in range(4):
         for lanes in range(4):
             wide[pl.ds(k * 16 + lanes, 4, stride=4), :] = orb_ref[k, :, lanes * 128 : lanes * 128 + 128].astype(
@@ -149,9 +145,11 @@
     for k in range(4):
         orb_mine[k] = wide[k * 16 : k * 16 + 16].astype(jnp.bfloat16)
 
+    pl.semaphore_wait(barrier, peers)
+
     def first_copy(d):
         return remote(
-            orb_mine, orb_all.at[pl.ds(4 * a, 4)], s1.at[d], r1.at[d], lax.rem(a + d + 1, ROWS), b
+            orb_mine, orb_all.at[pl.ds(4 * a, 4)], s1.at[0], r1.at[0], lax.rem(a + d + 1, ROWS), b
         )
 
     @pl.loop(0, ROWS - 1)
@@ -163,10 +161,10 @@
     def vec_first_copy(label):
         row, col = plane_owner(label)
         slot = 4 * side + b // 4
-        return remote(vec_ref, vec_got.at[slot], sva.at[label], rva.at[slot], row, col)
+        return remote(vec_ref, vec_got.at[slot], sva.at[0], rva.at[0], row, col)
 
     def vec_first_local():
-        return pltpu.make_async_copy(vec_ref, vec_got.at[4 * side + b // 4], lva)
+        return pltpu.make_async_copy(vec_ref, vec_got.at[4 * side + b // 4], rva.at[0])
 
     def screen_target(label):
         return lax.rem(label - residue + 8, 8), 2 * label + core
@@ -185,8 +183,7 @@
     def forward_copy(p):
         return remote(screen.at[p], screen.at[p], sf.at[p], rw.at[p], a, b + 1 - 2 * core)
 
-    @pl.loop(0, 32)
-    def _(i):
+    def screen_start(i):
         label = lax.rem(i + alpha, 8)
         turn = lax.rem(level - screen_target(label)[0] // 2 + 4, 4) == i // 8
 
@@ -197,6 +194,10 @@
         @pl.when(jnp.logical_and(turn, jnp.logical_not(screen_self(label))))
         def _():
             screen_copy(label).start()
+
+    @pl.loop(0, 16)
+    def _(i):
+        screen_start(i)
 
     @pl.loop(0, NK)
     def _(wanted):
@@ -205,9 +206,7 @@
             found = jnp.where(value[k] == wanted, k, found)
         place[wanted] = found
 
-    @pl.loop(0, ROWS - 1)
-    def _(d):
-        first_copy(d).wait()
+    remote(orb_all.at[pl.ds(0, 28)], orb_all.at[pl.ds(0, 28)], s1.at[0], r1.at[0], lax.rem(a + 1, ROWS), b).wait()
 
     @pl.loop(0, COLS)
     def _(dest):
@@ -218,11 +217,15 @@
 
     def second_copy(d):
         col = lax.rem(b + d + 1, COLS)
-        return remote(staged.at[col], landed.at[b], s2.at[d], r2.at[d], a, col)
+        return remote(staged.at[col], landed.at[b], s2.at[0], r2.at[0], a, col)
 
     @pl.loop(0, COLS - 1)
     def _(d):
         second_copy(d).start()
+
+    @pl.loop(16, 32)
+    def _(i):
+        screen_start(i)
 
     landed[b] = staged[b]
 
@@ -260,12 +263,13 @@
             p = slot * 4 + 1 - core + 2 * half
             forward_copy(p).wait_recv()
 
-    @pl.loop(0, 8)
-    def _(i):
-        row = lax.broadcasted_iota(jnp.int32, (128, PAIRS), 0) + i * 128
-        col = lax.broadcasted_iota(jnp.int32, (128, PAIRS), 1)
-        hit = jnp.logical_and((row & 31) == (col >> 5), (row >> 5) == (col & 31))
-        swap[pl.ds(pl.multiple_of(i * 128, 128), 128)] = jnp.where(hit, 1.0, 0.0).astype(jnp.bfloat16)
+    row = lax.broadcasted_iota(jnp.int32, (QUART, QUART), 0)
+    col = lax.broadcasted_iota(jnp.int32, (QUART, QUART), 1)
+    hit = jnp.logical_and((row & 31) == (col >> 3), (row >> 5) == (col & 7))
+    swap[...] = jnp.where(hit, 1.0, 0.0).astype(jnp.bfloat16)
+
+    def swapped(block):
+        return jnp.dot(block, swap[...], preferred_element_type=jnp.float32).astype(jnp.bfloat16)
 
     point = place[point_value]
     lane = lax.broadcasted_iota(jnp.int32, (8, QUART), 1)
@@ -277,9 +281,9 @@
         lower = jnp.where((lane >> 5) == v, energy[point, 8 * quarter + v], lower)
     gap[...] = upper - lower
 
-    @pl.loop(0, COLS - 1)
-    def _(d):
-        second_copy(d).wait()
+    remote(
+        staged.at[pl.ds(0, COLS - 1)], landed.at[pl.ds(0, COLS - 1)], s2.at[0], r2.at[0], a, lax.rem(b + 1, COLS)
+    ).wait()
 
     @pl.loop(0, 6)
     def _(slot):
@@ -298,14 +302,14 @@
         return remote(
             source,
             column.at[step, part_index],
-            sg.at[step, i],
-            rg.at[step, part_index],
+            sg.at[step],
+            rg.at[step],
             alpha,
             2 * lax.rem(alpha + i, 8) + spread_core,
         )
 
     def spread_local(step, source, p):
-        return pltpu.make_async_copy(source, column.at[step, p], lg.at[step])
+        return pltpu.make_async_copy(source, column.at[step, p], rg.at[step])
 
     def spread_self(i):
         return jnp.logical_and(i == 0, spread_own)
@@ -321,25 +325,15 @@
             def _():
                 spread_copy(step, source, i).start()
 
-    def spread_wait(step, source):
-        @pl.loop(0, 8)
-        def _(p):
-            here = jnp.logical_and(spread_own, p == part_index)
-
-            @pl.when(here)
-            def _():
-                spread_local(step, source, p).wait()
-
-            @pl.when(jnp.logical_not(here))
-            def _():
-                remote(
-                    source,
-                    column.at[step, p],
-                    sg.at[step, 0],
-                    rg.at[step, p],
-                    lax.rem(a + 1, ROWS),
-                    b,
-                ).wait_recv()
+    def spread_all(step, count):
+        return remote(
+            column.at[step, pl.ds(0, count)],
+            column.at[step, pl.ds(0, count)],
+            sg.at[step],
+            rg.at[step],
+            lax.rem(a + 1, ROWS),
+            b,
+        )
 
     wrap = jnp.where(alpha >= a, 0, 1)
     lane = lax.broadcasted_iota(jnp.int32, (32, 128), 1)
@@ -354,18 +348,31 @@
                 jnp.bfloat16
             )
         block = screen[pl.ds(slot * 4, 4)].reshape(NG, NG)
-        amplitude[...] = jnp.dot(valence[...], block, preferred_element_type=jnp.float32).astype(jnp.bfloat16)
-        for block in range(4):
-            product[...] = lax.dot_general(
-                amplitude[...],
+        for chunk in range(4):
+            rows = slice(chunk * 256, chunk * 256 + 256)
+            amplitude[rows] = jnp.dot(valence[rows], block, preferred_element_type=jnp.float32).astype(
+                jnp.bfloat16
+            )
+
+        def multiply(unit):
+            block, chunk = divmod(unit, 4)
+            product[unit % 2] = lax.dot_general(
+                amplitude[chunk * 256 : chunk * 256 + 256],
                 conduct[block * 256 : block * 256 + 256],
                 (((1,), (1,)), ((), ())),
                 preferred_element_type=jnp.float32,
             )
-            for octet in range(8):
+
+        def turn(unit):
+            block, chunk = divmod(unit, 4)
+            for octet in range(2):
                 for half in range(2):
                     s = [
-                        product[octet * 128 + i * 32 : octet * 128 + i * 32 + 32, half * 128 : half * 128 + 128]
+                        product[
+                            unit % 2,
+                            octet * 128 + i * 32 : octet * 128 + i * 32 + 32,
+                            half * 128 : half * 128 + 128,
+                        ]
                         for i in range(4)
                     ]
                     u0 = jnp.where(low, s[0], pltpu.roll(s[2], 64, 1))
@@ -378,12 +385,17 @@
                         jnp.where(even, u2, pltpu.roll(u3, 32, 1)),
                         jnp.where(even, pltpu.roll(u2, 96, 1), u3),
                     ]
-                    first = block * 256 + half * 128
-                    lanes = (octet % 2) * 128
-                    for i in range(4):
-                        tiles[m, octet // 2, t, first + i * 32 : first + i * 32 + 32, lanes : lanes + 128] = turned[
-                            i
-                        ].astype(jnp.bfloat16)
+                    for j in range(4):
+                        first = j * QUART + block * 64 + half * 32
+                        tiles[m, chunk, t, first : first + 32, octet * 128 : octet * 128 + 128] = jnp.concatenate(
+                            [turned[i][j * 8 : j * 8 + 8] for i in range(4)], axis=0
+                        ).astype(jnp.bfloat16)
+
+        multiply(0)
+        for unit in range(1, 16):
+            multiply(unit)
+            turn(unit - 1)
+        turn(15)
 
     arrive(level)
 
@@ -407,28 +419,25 @@
 
         @pl.when(phase == 1)
         def _():
-            @pl.loop(0, 8)
-            def _(i):
-                here = jnp.logical_and(plane_self, i == alpha)
-
-                @pl.when(jnp.logical_not(here))
-                def _():
-                    vec_first_copy(i).wait_send()
-
-            @pl.loop(0, 8)
-            def _(i):
-                here = jnp.logical_and(plane_self, i == 4 * side + b // 4)
-
-                @pl.when(here)
-                def _():
-                    vec_first_local().wait()
-
-                @pl.when(jnp.logical_not(here))
-                def _():
-                    remote(
-                        vec_ref, vec_got.at[i], sva.at[0], rva.at[i], lax.rem(a + 1, ROWS), b
-                    ).wait_recv()
-
+            def vec_all(count):
+                return remote(
+                    vec_got.at[pl.ds(0, count)],
+                    vec_got.at[pl.ds(0, count)],
+                    sva.at[0],
+                    rva.at[0],
+                    lax.rem(a + 1, ROWS),
+                    b,
+                )
+
+            @pl.when(plane_self)
+            def _():
+                vec_all(7).wait_send()
+
+            @pl.when(jnp.logical_not(plane_self))
+            def _():
+                vec_all(8).wait_send()
+
+            vec_all(8).wait_recv()
             for d in range(3):
                 home = alpha + 8 * lax.rem(level + d + 1, 4)
                 vec_sent[d] = vec_got[lax.rem(place[home], 8)]
@@ -440,7 +449,8 @@
             for d in range(3):
                 vec_second_copy(d).wait()
             own[...] = vec_row[place[point_value] // 8]
-            spread_start(0, own)
+            own_swapped[...] = swapped(own[...])
+            spread_start(0, own_swapped)
 
     @pl.loop(0, 8)
     def _(i):
@@ -460,45 +470,40 @@
 
     def partial_copy(step, index):
         row, col = peer(index)
-        return remote(sent.at[step, index], got.at[step, me], sp.at[step, index], rp.at[step, me], row, col)
-
-    def partial_arrival(step, index):
-        row, col = peer(index)
-        return remote(sent.at[step, index], got.at[step, index], sp.at[step, index], rp.at[step, index], row, col)
+        return remote(sent.at[step, index], got.at[step, me], sp.at[step], rp.at[step], row, col)
+
+    def partial_all(step):
+        return remote(
+            sent.at[step, pl.ds(0, COLS - 1)],
+            got.at[step, pl.ds(0, COLS - 1)],
+            sp.at[step],
+            rp.at[step],
+            lax.rem(a + 1, ROWS),
+            b,
+        )
 
     for step in range(3):
-        spread_wait(step, own if step == 0 else rounded.at[step - 1])
-        for t in range(2):
-            turned = jnp.zeros((NX, PAIRS), jnp.float32)
-            for j in range(4):
-                turned += jnp.dot(
-                    column[step, t * 4 + j],
-                    swap[j * QUART : j * QUART + QUART],
-                    preferred_element_type=jnp.float32,
-                )
-            ordered[:, t * PAIRS : t * PAIRS + PAIRS] = turned.astype(jnp.bfloat16)
+        spread_all(step, 8).wait_recv()
+        for p in range(8):
+            ordered[:, p * QUART : p * QUART + QUART] = column[step, p]
 
         @pl.loop(0, 4)
         def _(i):
             m = lax.rem(level + 1 + i, 4)
             for j in range(4):
-                index = 4 * m + j
-                sent[step, index] = jnp.dot(
+                sent[step, 4 * m + j] = jnp.dot(
                     ordered[...],
                     tiles[m, j].reshape(2 * PAIRS, QUART),
                     preferred_element_type=jnp.float32,
                 ).astype(jnp.bfloat16)
-
-                @pl.when(index != me)
+            for j in range(4):
+
+                @pl.when(4 * m + j != me)
                 def _():
-                    partial_copy(step, index).start()
+                    partial_copy(step, 4 * m + j).start()
 
         got[step, me] = sent[step, me]
-
-        @pl.loop(0, COLS - 1)
-        def _(d):
-            partial_arrival(step, lax.rem(me + d + 1, COLS)).wait_recv()
-
+        partial_all(step).wait_recv()
         total = jnp.zeros((NX, QUART), jnp.float32)
         for source in range(COLS):
             total += got[step, source].astype(jnp.float32)
@@ -511,39 +516,39 @@
         else:
             new = 2.0 * ((levels * state[1] + total) / SPREAD) - state[0]
         if step < 2:
-            rounded[step] = new.astype(jnp.bfloat16)
+            rounded[step] = swapped(new.astype(jnp.bfloat16))
             spread_start(step + 1, rounded.at[step])
         else:
             final_row[level] = new.astype(jnp.bfloat16)
 
     def row_copy(d):
         row = lax.rem(a + 2 * (d + 1), ROWS)
-        return remote(final_row.at[level], final_row.at[level], sa.at[d], ra.at[d], row, b)
+        return remote(final_row.at[level], final_row.at[level], sa.at[0], ra.at[0], row, b)
 
     for d in range(3):
         row_copy(d).start()
 
     for step in range(3):
-
-        @pl.loop(0, ROWS)
-        def _(i):
-            @pl.when(jnp.logical_not(spread_self(i)))
-            def _():
-                spread_copy(step, own if step == 0 else rounded.at[step - 1], i).wait_send()
-
-        @pl.loop(0, COLS - 1)
-        def _(d):
-            partial_copy(step, lax.rem(me + d + 1, COLS)).wait_send()
-
-    for d in range(3):
-        row_copy(d).wait()
+        partial_all(step).wait_send()
+
+        @pl.when(spread_own)
+        def _():
+            spread_all(step, 7).wait_send()
+
+        @pl.when(jnp.logical_not(spread_own))
+        def _():
+            spread_all(step, 8).wait_send()
+
+    remote(
+        final_row.at[pl.ds(0, 3)], final_row.at[pl.ds(0, 3)], sa.at[0], ra.at[0], lax.rem(a + 1, ROWS), b
+    ).wait()
 
     def last_copy(i):
         row, col = plane_device(i)
-        return remote(final_sent.at[i], final_got.at[alpha], sb.at[i], rb.at[alpha], row, col)
+        return remote(final_sent.at[i], final_got.at[alpha], sb.at[0], rb.at[0], row, col)
 
     def last_local(label):
-        return pltpu.make_async_copy(final_sent.at[4 * side + b // 4], final_got.at[label], lb)
+        return pltpu.make_async_copy(final_sent.at[4 * side + b // 4], final_got.at[label], rb.at[0])
 
     def last_self(i):
         return jnp.logical_and(plane_self, i == 4 * side + b // 4)
@@ -559,27 +564,26 @@
         def _():
             last_local(alpha).start()
 
-    @pl.loop(0, 8)
-    def _(label):
-        here = jnp.logical_and(plane_self, label == alpha)
-
-        @pl.when(here)
-        def _():
-            last_local(label).wait()
-
-        @pl.when(jnp.logical_not(here))
-        def _():
-            remote(
-                final_sent.at[0], final_got.at[label], sb.at[0], rb.at[label], lax.rem(a + 1, ROWS), b
-            ).wait_recv()
-
+    def last_all(count):
+        return remote(
+            final_sent.at[pl.ds(0, count)],
+            final_got.at[pl.ds(0, count)],
+            sb.at[0],
+            rb.at[0],
+            lax.rem(a + 1, ROWS),
+            b,
+        )
+
+    last_all(8).wait_recv()
     out_ref[...] = final_got[lax.rem(value[4 * a + b // 4], 8)].astype(jnp.float32)
 
-    @pl.loop(0, ROWS)
-    def _(i):
-        @pl.when(jnp.logical_not(last_self(i)))
-        def _():
-            last_copy(i).wait_send()
+    @pl.when(plane_self)
+    def _():
+        last_all(7).wait_send()
+
+    @pl.when(jnp.logical_not(plane_self))
+    def _():
+        last_all(8).wait_send()
 
 
 def per_device(orbitals, screened, kpoints, vectors, energies):
@@ -605,12 +609,13 @@
             pltpu.VMEM((PAIRS, NG), half),
             pltpu.VMEM((PAIRS, NG), half),
             pltpu.VMEM((PAIRS, NG), half),
-            pltpu.VMEM((PAIRS, 256), full),
+            pltpu.VMEM((2, 256, 256), full),
             pltpu.VMEM((4, 4, 2, PAIRS, QUART), half),
-            pltpu.VMEM((PAIRS, PAIRS), half),
+            pltpu.VMEM((QUART, QUART), half),
             pltpu.VMEM((4, NX, QUART), half),
             pltpu.VMEM((7, NX, QUART), half),
             pltpu.VMEM((8, NX, QUART), half),
+            pltpu.VMEM((NX, QUART), half),
             pltpu.VMEM((NX, QUART), half),
             pltpu.VMEM((8, QUART), full),
             pltpu.VMEM((3, 8, NX, QUART), half),
@@ -622,29 +627,26 @@
             pltpu.VMEM((4, NX, QUART), half),
             pltpu.VMEM((8, NX, QUART), half),
             pltpu.VMEM((8, NX, QUART), half),
-            dma((7,)),
-            dma((7,)),
-            dma((15,)),
-            dma((15,)),
+            dma((1,)),
+            dma((1,)),
+            dma((1,)),
+            dma((1,)),
             dma((8,)),
             dma((16,)),
             dma,
             dma((16,)),
-            dma((8,)),
-            dma((8,)),
-            dma,
+            dma((1,)),
+            dma((1,)),
             dma((3,)),
             dma((3,)),
-            dma((3, 8)),
-            dma((3, 8)),
-            dma((3,)),
-            dma((3, 16)),
-            dma((3, 16)),
             dma((3,)),
             dma((3,)),
-            dma((8,)),
-            dma((8,)),
-            dma,
+            dma((3,)),
+            dma((3,)),
+            dma((1,)),
+            dma((1,)),
+            dma((1,)),
+            dma((1,)),
         ],
         compiler_params=pltpu.CompilerParams(
             has_side_effects=True, collective_id=0, vmem_limit_bytes=56 << 20),

time: 119 us -> 112 us (0.941)
  Pallas kernels: 117 us -> 109 us
    pallas_call x1, Pallas kernels: 117 us -> 109 us  [per_device(): pl.pallas_call(kernel, out_shape=jax.ShapeDtypeStruct((NX, QUART), full),...]
where the time goes in v6:
time: 112 us; the launch traced here: 111 us
  Pallas kernels  109 us (97%)
  local copies, waits for them, and re-layouts  1.47 us (1%)
    pallas_call x1, Pallas kernels, per_device(): pl.pallas_call(kernel, out_shape=jax.ShapeDtypeStruct((NX, QUART), full),...  109 us

profile of v6, /device:TPU:0, one launch (start us, length us, event | category | flops | bytes accessed | tf_op | source)
XLA Modules:
  0.0 110.8 jit_solution(8957829744232261719)
XLA Ops:
  0.0 109.3 %mega.1 = f32[64,256]{1,0:T(8,128)} custom-call(s32[32]{0:T(128)} %value.1, f32[32,64]{1,0:T(8,128)} %energy.1, bf16[4,4,512]{2,1,0:T(4,128)(2,1)} %orb_ref.1, bf16[128,512]{1,0:T(8,128)(2,1)} %screen_ref.1, bf16[64,256]{1,0:T(8,128)(2,1)} %vec_ref.1), custom_call_target="tpu_custom_call" | custom-call | tf_op jit(solution)/shard_map/mega/pallas_call | solution.py:595
  109.3 1.5 %copy.7 = f32[64,256]{1,0:T(8,128)} copy(f32[64,256]{1,0:T(8,128)} %mega.1) | data formatting | bytes 131072

commit v7 on v6

--- a/solution.py
+++ b/solution.py
@@ -59,6 +59,8 @@
     ordered,
     sent,
     got,
+    pair_sent,
+    pair_got,
     rounded,
     state,
     final_row,
@@ -84,6 +86,8 @@
     ra,
     sb,
     rb,
+    ss,
+    rs,
 ):
     a = lax.axis_index("row")
     b = lax.axis_index("col")
@@ -96,7 +100,6 @@
     needed = lax.rem(alpha - a + 8, 8)
     quarter = 2 * side + core
     point_value = alpha + 8 * level
-    me = 2 * a + core
     plane_self = lax.rem(alpha, 2) == side
     spread_core = lax.rem(level, 2)
     spread_own = jnp.logical_and(alpha == a, spread_core == core)
@@ -120,7 +123,6 @@
     @pl.loop(0, ROWS - 1)
     def _(d):
         greet(lax.rem(a + d + 1, ROWS), b)
-        greet(lax.rem(a + d + 1, ROWS), b + 1 - 2 * core)
 
     @pl.loop(0, COLS - 1)
     def _(d):
@@ -133,7 +135,7 @@
         greet_other(*plane_owner(i))
         greet_other(4 * (i // 4) + 2 * core + lax.rem(i // 2, 2), 2 * a + lax.rem(i, 2))
 
-    peers = 2 * (ROWS - 1) + COLS - 1 + 32
+    peers = ROWS - 1 + COLS - 1 + 32
     peers -= jnp.where(needed == residue, 1, 0)
     peers -= jnp.where(plane_self, 2, 0)
     peers -= jnp.where(spread_own, 1, 0)
@@ -195,7 +197,7 @@
         def _():
             screen_copy(label).start()
 
-    @pl.loop(0, 16)
+    @pl.loop(0, 8)
     def _(i):
         screen_start(i)
 
@@ -223,7 +225,7 @@
     def _(d):
         second_copy(d).start()
 
-    @pl.loop(16, 32)
+    @pl.loop(8, 32)
     def _(i):
         screen_start(i)
 
@@ -403,14 +405,14 @@
     def _(phase):
         slot = lax.rem(level + phase, 4)
 
-        @pl.when(phase < 3)
-        def _():
-            arrive(lax.rem(slot + 1, 4))
-
         forwarded(slot)
 
         @pl.loop(0, 2)
         def _(t):
+            @pl.when(jnp.logical_and(t == 1, phase < 3))
+            def _():
+                arrive(lax.rem(slot + 1, 4))
+
             build(slot, lax.rem(slot + wrap + core + 2 * t, 4), t)
 
         @pl.when(phase == 0)
@@ -465,17 +467,23 @@
     mine = own[...].astype(jnp.float32)
     levels = gap[0:1]
 
-    def peer(index):
-        return index // 2, 2 * alpha + lax.rem(index, 2)
-
-    def partial_copy(step, index):
-        row, col = peer(index)
-        return remote(sent.at[step, index], got.at[step, me], sp.at[step], rp.at[step], row, col)
+    def pair_copy(step, m):
+        return remote(
+            pair_sent.at[step, m],
+            pair_got.at[step, m],
+            ss.at[step, m],
+            rs.at[step, m],
+            a,
+            b + 1 - 2 * core,
+        )
+
+    def partial_copy(step, row):
+        return remote(sent.at[step, row], got.at[step, a], sp.at[step], rp.at[step], row, b)
 
     def partial_all(step):
         return remote(
-            sent.at[step, pl.ds(0, COLS - 1)],
-            got.at[step, pl.ds(0, COLS - 1)],
+            sent.at[step, pl.ds(0, ROWS - 1)],
+            got.at[step, pl.ds(0, ROWS - 1)],
             sp.at[step],
             rp.at[step],
             lax.rem(a + 1, ROWS),
@@ -490,22 +498,38 @@
         @pl.loop(0, 4)
         def _(i):
             m = lax.rem(level + 1 + i, 4)
-            for j in range(4):
-                sent[step, 4 * m + j] = jnp.dot(
+            for half in range(2):
+                pair_sent[step, m, half] = jnp.dot(
                     ordered[...],
-                    tiles[m, j].reshape(2 * PAIRS, QUART),
+                    tiles[m, 2 * half + 1 - core].reshape(2 * PAIRS, QUART),
                     preferred_element_type=jnp.float32,
-                ).astype(jnp.bfloat16)
-            for j in range(4):
-
-                @pl.when(4 * m + j != me)
+                )
+            pair_copy(step, m).start()
+
+        @pl.loop(0, 4)
+        def _(i):
+            m = lax.rem(level + 1 + i, 4)
+            here = [
+                jnp.dot(
+                    ordered[...],
+                    tiles[m, 2 * half + core].reshape(2 * PAIRS, QUART),
+                    preferred_element_type=jnp.float32,
+                )
+                for half in range(2)
+            ]
+            pair_copy(step, m).wait_recv()
+            for half in range(2):
+                sent[step, 2 * m + half] = (here[half] + pair_got[step, m, half]).astype(jnp.bfloat16)
+            for half in range(2):
+
+                @pl.when(2 * m + half != a)
                 def _():
-                    partial_copy(step, 4 * m + j).start()
-
-        got[step, me] = sent[step, me]
+                    partial_copy(step, 2 * m + half).start()
+
+        got[step, a] = sent[step, a]
         partial_all(step).wait_recv()
         total = jnp.zeros((NX, QUART), jnp.float32)
-        for source in range(COLS):
+        for source in range(ROWS):
             total += got[step, source].astype(jnp.float32)
         if step == 0:
             new = (levels * mine + total) / SPREAD
@@ -530,6 +554,8 @@
 
     for step in range(3):
         partial_all(step).wait_send()
+        for m in range(4):
+            pair_copy(step, m).wait_send()
 
         @pl.when(spread_own)
         def _():
@@ -620,8 +646,10 @@
             pltpu.VMEM((8, QUART), full),
             pltpu.VMEM((3, 8, NX, QUART), half),
             pltpu.VMEM((NX, 2 * PAIRS), half),
-            pltpu.VMEM((3, COLS, NX, QUART), half),
-            pltpu.VMEM((3, COLS, NX, QUART), half),
+            pltpu.VMEM((3, ROWS, NX, QUART), half),
+            pltpu.VMEM((3, ROWS, NX, QUART), half),
+            pltpu.VMEM((3, 4, 2, NX, QUART), full),
+            pltpu.VMEM((3, 4, 2, NX, QUART), full),
             pltpu.VMEM((2, NX, QUART), half),
             pltpu.VMEM((2, NX, QUART), full),
             pltpu.VMEM((4, NX, QUART), half),
@@ -647,6 +675,8 @@
             dma((1,)),
             dma((1,)),
             dma((1,)),
+            dma((3, 4)),
+            dma((3, 4)),
         ],
         compiler_params=pltpu.CompilerParams(
             has_side_effects=True, collective_id=0, vmem_limit_bytes=56 << 20),

time: 112 us -> 107 us (0.955); the launches traced: 111 us -> 107 us
  Pallas kernels: 109 us -> 106 us
    pallas_call x1, Pallas kernels: 109 us -> 106 us  [per_device(): pl.pallas_call(kernel, out_shape=jax.ShapeDtypeStruct((NX, QUART), full),...]
where the time goes in v7:
time: 107 us
  Pallas kernels  106 us (99%)
  local copies, waits for them, and re-layouts  1.47 us (1%)
    pallas_call x1, Pallas kernels, per_device(): pl.pallas_call(kernel, out_shape=jax.ShapeDtypeStruct((NX, QUART), full),...  106 us

profile of v7, /device:TPU:0, one launch (start us, length us, event | category | flops | bytes accessed | tf_op | source)
XLA Modules:
  0.0 107.0 jit_solution(5053513687408218944)
XLA Ops:
  0.0 105.6 %mega.1 = f32[64,256]{1,0:T(8,128)} custom-call(s32[32]{0:T(128)} %value.1, f32[32,64]{1,0:T(8,128)} %energy.1, bf16[4,4,512]{2,1,0:T(4,128)(2,1)} %orb_ref.1, bf16[128,512]{1,0:T(8,128)(2,1)} %screen_ref.1, bf16[64,256]{1,0:T(8,128)(2,1)} %vec_ref.1), custom_call_target="tpu_custom_call" | custom-call | tf_op jit(solution)/shard_map/mega/pallas_call | solution.py:621
  105.6 1.5 %copy.7 = f32[64,256]{1,0:T(8,128)} copy(f32[64,256]{1,0:T(8,128)} %mega.1) | data formatting | bytes 131072

commit v8 on v7

--- a/solution.py
+++ b/solution.py
@@ -197,9 +197,6 @@
         def _():
             screen_copy(label).start()
 
-    @pl.loop(0, 8)
-    def _(i):
-        screen_start(i)
 
     @pl.loop(0, NK)
     def _(wanted):
@@ -225,7 +222,7 @@
     def _(d):
         second_copy(d).start()
 
-    @pl.loop(8, 32)
+    @pl.loop(0, 32)
     def _(i):
         screen_start(i)
 
@@ -495,8 +492,7 @@
         for p in range(8):
             ordered[:, p * QUART : p * QUART + QUART] = column[step, p]
 
-        @pl.loop(0, 4)
-        def _(i):
+        for i in range(4):
             m = lax.rem(level + 1 + i, 4)
             for half in range(2):
                 pair_sent[step, m, half] = jnp.dot(
@@ -506,8 +502,7 @@
                 )
             pair_copy(step, m).start()
 
-        @pl.loop(0, 4)
-        def _(i):
+        for i in range(4):
             m = lax.rem(level + 1 + i, 4)
             here = [
                 jnp.dot(
@@ -520,11 +515,9 @@
             pair_copy(step, m).wait_recv()
             for half in range(2):
                 sent[step, 2 * m + half] = (here[half] + pair_got[step, m, half]).astype(jnp.bfloat16)
-            for half in range(2):
-
-                @pl.when(2 * m + half != a)
-                def _():
+                if i < 3:
                     partial_copy(step, 2 * m + half).start()
+        partial_copy(step, a + 1 - 2 * side).start()
 
         got[step, a] = sent[step, a]
         partial_all(step).wait_recv()
@@ -621,7 +614,7 @@
     return pl.pallas_call(
         kernel,
         out_shape=jax.ShapeDtypeStruct((NX, QUART), full),
-        in_specs=[smem, smem, vmem, anywhere, anywhere],
+        in_specs=[smem, smem, vmem, vmem, anywhere],
         out_specs=vmem,
         scratch_shapes=[
             pltpu.SMEM((NK,), jnp.int32),

time: 107 us -> 106 us (level)
  no operation moved by 1% of the time
where the time goes in v8:
time: 106 us
  Pallas kernels  105 us (99%)
  local copies, waits for them, and re-layouts  1.47 us (1%)
    pallas_call x1, Pallas kernels, per_device(): pl.pallas_call(kernel, out_shape=jax.ShapeDtypeStruct((NX, QUART), full),...  105 us

profile of v8, /device:TPU:0, one launch (start us, length us, event | category | flops | bytes accessed | tf_op | source)
XLA Modules:
  0.0 106.3 jit_solution(13226452624864711920)
XLA Ops:
  0.0 104.8 %mega.1 = f32[64,256]{1,0:T(8,128)} custom-call(s32[32]{0:T(128)} %value.1, f32[32,64]{1,0:T(8,128)} %energy.1, bf16[4,4,512]{2,1,0:T(4,128)(2,1)} %orb_ref.1, bf16[128,512]{1,0:T(8,128)(2,1)} %screen_ref.1, bf16[64,256]{1,0:T(8,128)(2,1)} %vec_ref.1), custom_call_target="tpu_custom_call" | custom-call | tf_op jit(solution)/shard_map/mega/pallas_call | solution.py:614
  104.8 1.5 %copy.7 = f32[64,256]{1,0:T(8,128)} copy(f32[64,256]{1,0:T(8,128)} %mega.1) | data formatting | bytes 131072

commit v9 on v8

--- a/solution.py
+++ b/solution.py
@@ -493,7 +493,7 @@
             ordered[:, p * QUART : p * QUART + QUART] = column[step, p]
 
         for i in range(4):
-            m = lax.rem(level + 1 + i, 4)
+            m = lax.rem(level + (2, 1, 3, 0)[i], 4)
             for half in range(2):
                 pair_sent[step, m, half] = jnp.dot(
                     ordered[...],
@@ -503,7 +503,7 @@
             pair_copy(step, m).start()
 
         for i in range(4):
-            m = lax.rem(level + 1 + i, 4)
+            m = lax.rem(level + (2, 1, 3, 0)[i], 4)
             here = [
                 jnp.dot(
                     ordered[...],

time: 106 us -> 106 us (level)
  no operation moved by 1% of the time
where the time goes in v9:
time: 106 us
  Pallas kernels  104 us (98%)
  local copies, waits for them, and re-layouts  1.47 us (1%)
    pallas_call x1, Pallas kernels, per_device(): pl.pallas_call(kernel, out_shape=jax.ShapeDtypeStruct((NX, QUART), full),...  104 us

profile of v9, /device:TPU:0, one launch (start us, length us, event | category | flops | bytes accessed | tf_op | source)
XLA Modules:
  0.0 105.8 jit_solution(7476442619217747031)
XLA Ops:
  0.0 104.4 %mega.1 = f32[64,256]{1,0:T(8,128)} custom-call(s32[32]{0:T(128)} %value.1, f32[32,64]{1,0:T(8,128)} %energy.1, bf16[4,4,512]{2,1,0:T(4,128)(2,1)} %orb_ref.1, bf16[128,512]{1,0:T(8,128)(2,1)} %screen_ref.1, bf16[64,256]{1,0:T(8,128)(2,1)} %vec_ref.1), custom_call_target="tpu_custom_call" | custom-call | tf_op jit(solution)/shard_map/mega/pallas_call | solution.py:614
  104.4 1.5 %copy.7 = f32[64,256]{1,0:T(8,128)} copy(f32[64,256]{1,0:T(8,128)} %mega.1) | data formatting | bytes 131072
